TPU v7x, 512 devices: a whole 4x8x8 slice. The times are simulated.
512 devices in a mesh: blk: 16 (over x_hi, z), grp: 32 (over y, x_lo, core).
Axes of the slice: x: 4 (x_hi: 2, x_lo: 2; x = x_hi * 2 + x_lo), y: 8, z: 8, core: 2. Of those that a mesh axis runs over, the one named last changes fastest.
Arguments:
- position: float32 [3, 262144], P(None, ('blk', 'grp')), may hold values from -6 to 6
- velocity: float32 [3, 262144], P(None, ('blk', 'grp')), may hold values from -6 to 6
- accel_old: float32 [3, 262144], P(None, ('blk', 'grp')), may hold values from -6 to 6
- jerk_old: float32 [3, 262144], P(None, ('blk', 'grp')), may hold values from -6 to 6
- mass: float32 [262144], P(('blk', 'grp')), may hold values from 1e-07 to 1e-05
- elapsed: float32 [262144], P(('blk', 'grp')), may hold values from 0.1 to 1
- active_index: int32 [8192], P(('blk', 'grp')), may hold values from 0 to 262143, as said below
Outputs:
- predicted: float32 [6, 262144], P(None, ('blk', 'grp'))
- accel: float32 [3, 8192], P(None, ('blk', 'grp'))
- jerk: float32 [3, 8192], P(None, ('blk', 'grp'))
Inputs may be any that keep to these rules, and one draw needn't show every extreme that they name: `active_index`: entries 16 * k to 16 * k + 15 are distinct stars of the range 512 * k to 512 * k + 511, for every k.
All inputs are finite; a program needn't handle non-finite values.
Results may differ from a plain program's by a relative error of at most 0.0003.
Values sent between devices are 32-bit elements; how exact they have to be, the bound alone decides.
No kernel may reach another device: no remote copies, remote signals or barrier semaphores. Data moves between devices by JAX's collectives and lax.ppermute only.
A program may use at most 64 MiB of HBM per device.

v0:
```python
import math

import jax
import jax.numpy as jnp
from jax import lax
from jax.sharding import PartitionSpec as P

SOFTENING = 0.0001


def joined_along(parts, dim):
    lengths = list(parts.shape[1:])
    lengths[dim] *= parts.shape[0]
    return jnp.moveaxis(parts, 0, dim).reshape(lengths)


def copy_for_each(shard, axis):
    count = lax.axis_size(axis)
    return lax.all_to_all(
        jnp.broadcast_to(shard[None], (count, *shard.shape)), axis, 0, 0, tiled=True
    )


def gather_directly(shard, axis, dim):
    return joined_along(copy_for_each(shard, axis), dim)


def from_behind(shard, axis, by):
    count = lax.axis_size(axis)
    return lax.ppermute(shard, axis, [(i, (i + by) % count) for i in range(count)])


def cut_along(shard, dim, count):
    lengths = shard.shape
    parts = shard.reshape(*lengths[:dim], count, lengths[dim] // count, *lengths[dim + 1 :])
    return jnp.moveaxis(parts, dim, 0)


def sent_and_summed(shard, axis, dim):
    parts = cut_along(shard, dim, lax.axis_size(axis))
    arrived = lax.all_to_all(parts, axis, split_axis=0, concat_axis=0, tiled=True)
    return arrived.sum(axis=0)


def predict(position, velocity, accel_old, jerk_old, elapsed):
    step_row = elapsed[None, :]
    half = step_row * step_row * 0.5
    sixth = half * step_row * (1.0 / 3.0)
    new_position = position + step_row * velocity + half * accel_old + sixth * jerk_old
    new_velocity = velocity + step_row * accel_old + half * jerk_old
    return jnp.concatenate([new_position, new_velocity], 0)


def interact(targets, sources, masses):
    columns = targets.shape[1]
    block_size = math.gcd(columns, 128)
    blocks = columns // block_size
    stacked = targets.reshape(6, blocks, block_size).transpose(1, 0, 2)

    def one_block(target_block):
        separation = sources[0:3][:, None, :] - target_block[0:3][:, :, None]
        relative = sources[3:6][:, None, :] - target_block[3:6][:, :, None]
        distance = jnp.sum(separation * separation, 0) + SOFTENING
        inverse = 1.0 / jnp.sqrt(distance)
        weight = masses[None, :] * inverse * inverse * inverse
        radial = 3.0 * jnp.sum(separation * relative, 0) / distance
        accel_part = jnp.sum(weight[None] * separation, 2)
        jerk_part = jnp.sum(weight[None] * (relative - radial[None] * separation), 2)
        return jnp.concatenate([accel_part, jerk_part], 0)

    result = lax.map(one_block, stacked)
    return result.transpose(1, 0, 2).reshape(6, columns)


def local(position, velocity, accel_old, jerk_old, mass, elapsed, active_index):
    predicted = predict(position, velocity, accel_old, jerk_old, elapsed)
    stars_here = position.shape[1]
    device = lax.axis_index("blk") * lax.axis_size("grp") + lax.axis_index("grp")
    offsets = active_index - device * stars_here
    owned_rows = jnp.take(predicted, offsets, axis=1)
    group_rows = gather_directly(owned_rows, "grp", 1)

    def circulate(number, carry):
        visitor, partial_value = carry
        partial_value = partial_value + interact(visitor, predicted, mass)
        return from_behind((visitor, partial_value), "blk", 1)

    start = jnp.zeros(group_rows.shape, jnp.float32)
    visitor, partial_value = lax.fori_loop(0, lax.axis_size("blk"), circulate, (group_rows, start))
    owned = sent_and_summed(partial_value, "grp", 1)
    return (predicted, owned[0:3], owned[3:6])


def solution(mesh):
    in_specs = (
        P(None, ("blk", "grp")),
        P(None, ("blk", "grp")),
        P(None, ("blk", "grp")),
        P(None, ("blk", "grp")),
        P(("blk", "grp")),
        P(("blk", "grp")),
        P(("blk", "grp")),
    )
    out_specs = (P(None, ("blk", "grp")), P(None, ("blk", "grp")), P(None, ("blk", "grp")))
    return jax.shard_map(local, mesh=mesh, in_specs=in_specs, out_specs=out_specs, check_vma=False)
```

profile of v0, /device:TPU:1, one launch (start us, length us, event | category | flops | bytes accessed | tf_op | source)
XLA Modules:
  0.0 272.2 jit_solution(2226634823596071155)
XLA Ops:
  5.4 10.3 %all-to-all-start = ((f32[32,6,16]{2,1,0:T(8,128)}), f32[32,6,16]{2,1,0:T(8,128)S(1)}, u32[]{:S(2)}, u32[]{:S(2)}) async-start(f32[32,6,16]{2,1,0:T(8,128)} %broadcast_in_dim.37), calls=%async_computation | async-start | bytes 262144 | tf_op jit(solution)/shard_map/all_to_all | solution.py:19
  15.8 9.4 %all-to-all-done = f32[32,6,16]{2,1,0:T(8,128)S(1)} async-done(((f32[32,6,16]{2,1,0:T(8,128)}), f32[32,6,16]{2,1,0:T(8,128)S(1)}, u32[]{:S(2)}, u32[]{:S(2)}) %all-to-all-start) | async-done | bytes 12320 | tf_op jit(solution)/shard_map/all_to_all | solution.py:19
  26.0 215.6 %while.23 = (s32[]{:T(128)}, f32[6,512]{1,0:T(8,128)S(1)}, f32[6,512]{1,0:T(8,128)S(1)}, f32[3,512]{1,0:T(4,128)S(1)}, f32[512]{0:T(512)S(1)}, /*index=5*/f32[3,...) while((s32[]{:T(128)}, f32[6,512]{1,0:T(8,128)S(1)}, f32[6,512]{1,0:T(8,128)S(1)}, ...), condition=%wide.region_7.8_spmd, body=%wide.region_0.7_spmd.sunk | while | flops 3017732 | bytes 2313546 | solution.py:89
  26.0 3.0 %while.24 = (s32[]{:T(128)}, f32[4,6,128]{2,1,0:T(8,128)S(1)}, f32[3,512]{1,0:T(4,128)S(1)}, f32[4,6,128]{2,1,0:T(8,128)S(1)}, f32[512]{0:T(512)S(1)}, /*index=5*/f32[3,512]{1,0:T(4,128)S(1)}, s32[]{:T(128)}) while((s32[]{:T(128)}, f32[4,6,128]{2,1,0:T(8,128)S(1)}, f32[3,512]{1,0:T(4,128)S(1)}, f32[4,6,128]{2,1,0:T(8,128)S(1)}, ...), condition=%wide.region_6.6_spmd, body=%wide.region_1.5_spmd.sunk | while | flops 3014658 | bytes 2153557 | solution.py:71
  29.1 3.1 %collective-permute-start.1 = (f32[6,512]{1,0:T(8,128)S(1)}, f32[6,512]{1,0:T(8,128)S(1)}, u32[]{:S(2)}, u32[]{:S(2)}) collective-permute-start(f32[6,512]{1,0:T(8,128)S(1)} %bitcast_add_fusion.2), channel_id=1, source_target_pairs={{0,32},{32,64},{64,96},{96,128},{128,160},{160,192},{192,224},{224... | collective-permute-start | bytes 36872 | tf_op jit(solution)/shard_map/while/body/eval_jaxpr/ppermute | solution.py:30
  32.2 4.0 %collective-permute-start = (f32[6,512]{1,0:T(8,128)S(1)}, f32[6,512]{1,0:T(8,128)S(1)}, u32[]{:S(2)}, u32[]{:S(2)}) collective-permute-start(f32[6,512]{1,0:T(8,128)S(1)} %bitcast.28), channel_id=1, source_target_pairs={{0,32},{32,64},{64,96},{96,128},{128,160},{160,192},{192,224},{224... | collective-permute-start | bytes 36872 | tf_op jit(solution)/shard_map/while/body/eval_jaxpr/ppermute | solution.py:30
  36.3 5.9 %collective-permute-done.1 = f32[6,512]{1,0:T(8,128)S(1)} collective-permute-done((f32[6,512]{1,0:T(8,128)S(1)}, f32[6,512]{1,0:T(8,128)S(1)}, u32[]{:S(2)}, u32[]{:S(2)}) %collective-permute-start.1) | collective-permute-done | bytes 12320 | tf_op jit(solution)/shard_map/while/body/eval_jaxpr/ppermute | solution.py:30
  42.2 1.9 collective-permute-done
  44.1 3.0 %while.24 = (s32[]{:T(128)}, f32[4,6,128]{2,1,0:T(8,128)S(1)}, f32[3,512]{1,0:T(4,128)S(1)}, f32[4,6,128]{2,1,0:T(8,128)S(1)}, f32[512]{0:T(512)S(1)}, /*index=5*/f32[3,512]{1,0:T(4,128)S(1)}, s32[]{:T(128)}) while((s32[]{:T(128)}, f32[4,6,128]{2,1,0:T(8,128)S(1)}, f32[3,512]{1,0:T(4,128)S(1)}, f32[4,6,128]{2,1,0:T(8,128)S(1)}, ...), condition=%wide.region_6.6_spmd, body=%wide.region_1.5_spmd.sunk | while | flops 3014658 | bytes 2153557 | solution.py:71
  51.1 4.2 %collective-permute-done.1 = f32[6,512]{1,0:T(8,128)S(1)} collective-permute-done((f32[6,512]{1,0:T(8,128)S(1)}, f32[6,512]{1,0:T(8,128)S(1)}, u32[]{:S(2)}, u32[]{:S(2)}) %collective-permute-start.1) | collective-permute-done | bytes 12320 | tf_op jit(solution)/shard_map/while/body/eval_jaxpr/ppermute | solution.py:30
  55.3 2.1 collective-permute-done
  57.4 3.0 %while.24 = (s32[]{:T(128)}, f32[4,6,128]{2,1,0:T(8,128)S(1)}, f32[3,512]{1,0:T(4,128)S(1)}, f32[4,6,128]{2,1,0:T(8,128)S(1)}, f32[512]{0:T(512)S(1)}, /*index=5*/f32[3,512]{1,0:T(4,128)S(1)}, s32[]{:T(128)}) while((s32[]{:T(128)}, f32[4,6,128]{2,1,0:T(8,128)S(1)}, f32[3,512]{1,0:T(4,128)S(1)}, f32[4,6,128]{2,1,0:T(8,128)S(1)}, ...), condition=%wide.region_6.6_spmd, body=%wide.region_1.5_spmd.sunk | while | flops 3014658 | bytes 2153557 | solution.py:71
  64.3 4.2 %collective-permute-done.1 = f32[6,512]{1,0:T(8,128)S(1)} collective-permute-done((f32[6,512]{1,0:T(8,128)S(1)}, f32[6,512]{1,0:T(8,128)S(1)}, u32[]{:S(2)}, u32[]{:S(2)}) %collective-permute-start.1) | collective-permute-done | bytes 12320 | tf_op jit(solution)/shard_map/while/body/eval_jaxpr/ppermute | solution.py:30
  70.5 3.0 %while.24 = (s32[]{:T(128)}, f32[4,6,128]{2,1,0:T(8,128)S(1)}, f32[3,512]{1,0:T(4,128)S(1)}, f32[4,6,128]{2,1,0:T(8,128)S(1)}, f32[512]{0:T(512)S(1)}, /*index=5*/f32[3,512]{1,0:T(4,128)S(1)}, s32[]{:T(128)}) while((s32[]{:T(128)}, f32[4,6,128]{2,1,0:T(8,128)S(1)}, f32[3,512]{1,0:T(4,128)S(1)}, f32[4,6,128]{2,1,0:T(8,128)S(1)}, ...), condition=%wide.region_6.6_spmd, body=%wide.region_1.5_spmd.sunk | while | flops 3014658 | bytes 2153557 | solution.py:71
  77.4 4.2 %collective-permute-done.1 = f32[6,512]{1,0:T(8,128)S(1)} collective-permute-done((f32[6,512]{1,0:T(8,128)S(1)}, f32[6,512]{1,0:T(8,128)S(1)}, u32[]{:S(2)}, u32[]{:S(2)}) %collective-permute-start.1) | collective-permute-done | bytes 12320 | tf_op jit(solution)/shard_map/while/body/eval_jaxpr/ppermute | solution.py:30
  81.7 1.9 collective-permute-done
  83.6 3.0 %while.24 = (s32[]{:T(128)}, f32[4,6,128]{2,1,0:T(8,128)S(1)}, f32[3,512]{1,0:T(4,128)S(1)}, f32[4,6,128]{2,1,0:T(8,128)S(1)}, f32[512]{0:T(512)S(1)}, /*index=5*/f32[3,512]{1,0:T(4,128)S(1)}, s32[]{:T(128)}) while((s32[]{:T(128)}, f32[4,6,128]{2,1,0:T(8,128)S(1)}, f32[3,512]{1,0:T(4,128)S(1)}, f32[4,6,128]{2,1,0:T(8,128)S(1)}, ...), condition=%wide.region_6.6_spmd, body=%wide.region_1.5_spmd.sunk | while | flops 3014658 | bytes 2153557 | solution.py:71
  90.5 4.2 %collective-permute-done.1 = f32[6,512]{1,0:T(8,128)S(1)} collective-permute-done((f32[6,512]{1,0:T(8,128)S(1)}, f32[6,512]{1,0:T(8,128)S(1)}, u32[]{:S(2)}, u32[]{:S(2)}) %collective-permute-start.1) | collective-permute-done | bytes 12320 | tf_op jit(solution)/shard_map/while/body/eval_jaxpr/ppermute | solution.py:30
  94.7 1.9 collective-permute-done
  96.7 3.0 %while.24 = (s32[]{:T(128)}, f32[4,6,128]{2,1,0:T(8,128)S(1)}, f32[3,512]{1,0:T(4,128)S(1)}, f32[4,6,128]{2,1,0:T(8,128)S(1)}, f32[512]{0:T(512)S(1)}, /*index=5*/f32[3,512]{1,0:T(4,128)S(1)}, s32[]{:T(128)}) while((s32[]{:T(128)}, f32[4,6,128]{2,1,0:T(8,128)S(1)}, f32[3,512]{1,0:T(4,128)S(1)}, f32[4,6,128]{2,1,0:T(8,128)S(1)}, ...), condition=%wide.region_6.6_spmd, body=%wide.region_1.5_spmd.sunk | while | flops 3014658 | bytes 2153557 | solution.py:71
  103.6 4.2 %collective-permute-done.1 = f32[6,512]{1,0:T(8,128)S(1)} collective-permute-done((f32[6,512]{1,0:T(8,128)S(1)}, f32[6,512]{1,0:T(8,128)S(1)}, u32[]{:S(2)}, u32[]{:S(2)}) %collective-permute-start.1) | collective-permute-done | bytes 12320 | tf_op jit(solution)/shard_map/while/body/eval_jaxpr/ppermute | solution.py:30
  107.8 1.9 collective-permute-done
  109.8 3.0 %while.24 = (s32[]{:T(128)}, f32[4,6,128]{2,1,0:T(8,128)S(1)}, f32[3,512]{1,0:T(4,128)S(1)}, f32[4,6,128]{2,1,0:T(8,128)S(1)}, f32[512]{0:T(512)S(1)}, /*index=5*/f32[3,512]{1,0:T(4,128)S(1)}, s32[]{:T(128)}) while((s32[]{:T(128)}, f32[4,6,128]{2,1,0:T(8,128)S(1)}, f32[3,512]{1,0:T(4,128)S(1)}, f32[4,6,128]{2,1,0:T(8,128)S(1)}, ...), condition=%wide.region_6.6_spmd, body=%wide.region_1.5_spmd.sunk | while | flops 3014658 | bytes 2153557 | solution.py:71
  116.7 4.2 %collective-permute-done.1 = f32[6,512]{1,0:T(8,128)S(1)} collective-permute-done((f32[6,512]{1,0:T(8,128)S(1)}, f32[6,512]{1,0:T(8,128)S(1)}, u32[]{:S(2)}, u32[]{:S(2)}) %collective-permute-start.1) | collective-permute-done | bytes 12320 | tf_op jit(solution)/shard_map/while/body/eval_jaxpr/ppermute | solution.py:30
  122.9 3.0 %while.24 = (s32[]{:T(128)}, f32[4,6,128]{2,1,0:T(8,128)S(1)}, f32[3,512]{1,0:T(4,128)S(1)}, f32[4,6,128]{2,1,0:T(8,128)S(1)}, f32[512]{0:T(512)S(1)}, /*index=5*/f32[3,512]{1,0:T(4,128)S(1)}, s32[]{:T(128)}) while((s32[]{:T(128)}, f32[4,6,128]{2,1,0:T(8,128)S(1)}, f32[3,512]{1,0:T(4,128)S(1)}, f32[4,6,128]{2,1,0:T(8,128)S(1)}, ...), condition=%wide.region_6.6_spmd, body=%wide.region_1.5_spmd.sunk | while | flops 3014658 | bytes 2153557 | solution.py:71
  129.8 4.2 %collective-permute-done.1 = f32[6,512]{1,0:T(8,128)S(1)} collective-permute-done((f32[6,512]{1,0:T(8,128)S(1)}, f32[6,512]{1,0:T(8,128)S(1)}, u32[]{:S(2)}, u32[]{:S(2)}) %collective-permute-start.1) | collective-permute-done | bytes 12320 | tf_op jit(solution)/shard_map/while/body/eval_jaxpr/ppermute | solution.py:30
  134.0 1.9 collective-permute-done
  136.0 3.0 %while.24 = (s32[]{:T(128)}, f32[4,6,128]{2,1,0:T(8,128)S(1)}, f32[3,512]{1,0:T(4,128)S(1)}, f32[4,6,128]{2,1,0:T(8,128)S(1)}, f32[512]{0:T(512)S(1)}, /*index=5*/f32[3,512]{1,0:T(4,128)S(1)}, s32[]{:T(128)}) while((s32[]{:T(128)}, f32[4,6,128]{2,1,0:T(8,128)S(1)}, f32[3,512]{1,0:T(4,128)S(1)}, f32[4,6,128]{2,1,0:T(8,128)S(1)}, ...), condition=%wide.region_6.6_spmd, body=%wide.region_1.5_spmd.sunk | while | flops 3014658 | bytes 2153557 | solution.py:71
  142.9 4.2 %collective-permute-done.1 = f32[6,512]{1,0:T(8,128)S(1)} collective-permute-done((f32[6,512]{1,0:T(8,128)S(1)}, f32[6,512]{1,0:T(8,128)S(1)}, u32[]{:S(2)}, u32[]{:S(2)}) %collective-permute-start.1) | collective-permute-done | bytes 12320 | tf_op jit(solution)/shard_map/while/body/eval_jaxpr/ppermute | solution.py:30
  147.1 1.9 collective-permute-done
  149.1 3.0 %while.24 = (s32[]{:T(128)}, f32[4,6,128]{2,1,0:T(8,128)S(1)}, f32[3,512]{1,0:T(4,128)S(1)}, f32[4,6,128]{2,1,0:T(8,128)S(1)}, f32[512]{0:T(512)S(1)}, /*index=5*/f32[3,512]{1,0:T(4,128)S(1)}, s32[]{:T(128)}) while((s32[]{:T(128)}, f32[4,6,128]{2,1,0:T(8,128)S(1)}, f32[3,512]{1,0:T(4,128)S(1)}, f32[4,6,128]{2,1,0:T(8,128)S(1)}, ...), condition=%wide.region_6.6_spmd, body=%wide.region_1.5_spmd.sunk | while | flops 3014658 | bytes 2153557 | solution.py:71
  156.0 4.2 %collective-permute-done.1 = f32[6,512]{1,0:T(8,128)S(1)} collective-permute-done((f32[6,512]{1,0:T(8,128)S(1)}, f32[6,512]{1,0:T(8,128)S(1)}, u32[]{:S(2)}, u32[]{:S(2)}) %collective-permute-start.1) | collective-permute-done | bytes 12320 | tf_op jit(solution)/shard_map/while/body/eval_jaxpr/ppermute | solution.py:30
  162.2 3.0 %while.24 = (s32[]{:T(128)}, f32[4,6,128]{2,1,0:T(8,128)S(1)}, f32[3,512]{1,0:T(4,128)S(1)}, f32[4,6,128]{2,1,0:T(8,128)S(1)}, f32[512]{0:T(512)S(1)}, /*index=5*/f32[3,512]{1,0:T(4,128)S(1)}, s32[]{:T(128)}) while((s32[]{:T(128)}, f32[4,6,128]{2,1,0:T(8,128)S(1)}, f32[3,512]{1,0:T(4,128)S(1)}, f32[4,6,128]{2,1,0:T(8,128)S(1)}, ...), condition=%wide.region_6.6_spmd, body=%wide.region_1.5_spmd.sunk | while | flops 3014658 | bytes 2153557 | solution.py:71
  169.1 4.2 %collective-permute-done.1 = f32[6,512]{1,0:T(8,128)S(1)} collective-permute-done((f32[6,512]{1,0:T(8,128)S(1)}, f32[6,512]{1,0:T(8,128)S(1)}, u32[]{:S(2)}, u32[]{:S(2)}) %collective-permute-start.1) | collective-permute-done | bytes 12320 | tf_op jit(solution)/shard_map/while/body/eval_jaxpr/ppermute | solution.py:30
  173.3 1.9 collective-permute-done
  175.3 3.0 %while.24 = (s32[]{:T(128)}, f32[4,6,128]{2,1,0:T(8,128)S(1)}, f32[3,512]{1,0:T(4,128)S(1)}, f32[4,6,128]{2,1,0:T(8,128)S(1)}, f32[512]{0:T(512)S(1)}, /*index=5*/f32[3,512]{1,0:T(4,128)S(1)}, s32[]{:T(128)}) while((s32[]{:T(128)}, f32[4,6,128]{2,1,0:T(8,128)S(1)}, f32[3,512]{1,0:T(4,128)S(1)}, f32[4,6,128]{2,1,0:T(8,128)S(1)}, ...), condition=%wide.region_6.6_spmd, body=%wide.region_1.5_spmd.sunk | while | flops 3014658 | bytes 2153557 | solution.py:71
  182.2 4.2 %collective-permute-done.1 = f32[6,512]{1,0:T(8,128)S(1)} collective-permute-done((f32[6,512]{1,0:T(8,128)S(1)}, f32[6,512]{1,0:T(8,128)S(1)}, u32[]{:S(2)}, u32[]{:S(2)}) %collective-permute-start.1) | collective-permute-done | bytes 12320 | tf_op jit(solution)/shard_map/while/body/eval_jaxpr/ppermute | solution.py:30
  186.4 1.9 collective-permute-done
  188.4 3.0 %while.24 = (s32[]{:T(128)}, f32[4,6,128]{2,1,0:T(8,128)S(1)}, f32[3,512]{1,0:T(4,128)S(1)}, f32[4,6,128]{2,1,0:T(8,128)S(1)}, f32[512]{0:T(512)S(1)}, /*index=5*/f32[3,512]{1,0:T(4,128)S(1)}, s32[]{:T(128)}) while((s32[]{:T(128)}, f32[4,6,128]{2,1,0:T(8,128)S(1)}, f32[3,512]{1,0:T(4,128)S(1)}, f32[4,6,128]{2,1,0:T(8,128)S(1)}, ...), condition=%wide.region_6.6_spmd, body=%wide.region_1.5_spmd.sunk | while | flops 3014658 | bytes 2153557 | solution.py:71
  195.3 4.7 %collective-permute-done.1 = f32[6,512]{1,0:T(8,128)S(1)} collective-permute-done((f32[6,512]{1,0:T(8,128)S(1)}, f32[6,512]{1,0:T(8,128)S(1)}, u32[]{:S(2)}, u32[]{:S(2)}) %collective-permute-start.1) | collective-permute-done | bytes 12320 | tf_op jit(solution)/shard_map/while/body/eval_jaxpr/ppermute | solution.py:30
  201.9 3.0 %while.24 = (s32[]{:T(128)}, f32[4,6,128]{2,1,0:T(8,128)S(1)}, f32[3,512]{1,0:T(4,128)S(1)}, f32[4,6,128]{2,1,0:T(8,128)S(1)}, f32[512]{0:T(512)S(1)}, /*index=5*/f32[3,512]{1,0:T(4,128)S(1)}, s32[]{:T(128)}) while((s32[]{:T(128)}, f32[4,6,128]{2,1,0:T(8,128)S(1)}, f32[3,512]{1,0:T(4,128)S(1)}, f32[4,6,128]{2,1,0:T(8,128)S(1)}, ...), condition=%wide.region_6.6_spmd, body=%wide.region_1.5_spmd.sunk | while | flops 3014658 | bytes 2153557 | solution.py:71
  208.9 4.2 %collective-permute-done.1 = f32[6,512]{1,0:T(8,128)S(1)} collective-permute-done((f32[6,512]{1,0:T(8,128)S(1)}, f32[6,512]{1,0:T(8,128)S(1)}, u32[]{:S(2)}, u32[]{:S(2)}) %collective-permute-start.1) | collective-permute-done | bytes 12320 | tf_op jit(solution)/shard_map/while/body/eval_jaxpr/ppermute | solution.py:30
  215.0 3.0 %while.24 = (s32[]{:T(128)}, f32[4,6,128]{2,1,0:T(8,128)S(1)}, f32[3,512]{1,0:T(4,128)S(1)}, f32[4,6,128]{2,1,0:T(8,128)S(1)}, f32[512]{0:T(512)S(1)}, /*index=5*/f32[3,512]{1,0:T(4,128)S(1)}, s32[]{:T(128)}) while((s32[]{:T(128)}, f32[4,6,128]{2,1,0:T(8,128)S(1)}, f32[3,512]{1,0:T(4,128)S(1)}, f32[4,6,128]{2,1,0:T(8,128)S(1)}, ...), condition=%wide.region_6.6_spmd, body=%wide.region_1.5_spmd.sunk | while | flops 3014658 | bytes 2153557 | solution.py:71
  221.9 4.2 %collective-permute-done.1 = f32[6,512]{1,0:T(8,128)S(1)} collective-permute-done((f32[6,512]{1,0:T(8,128)S(1)}, f32[6,512]{1,0:T(8,128)S(1)}, u32[]{:S(2)}, u32[]{:S(2)}) %collective-permute-start.1) | collective-permute-done | bytes 12320 | tf_op jit(solution)/shard_map/while/body/eval_jaxpr/ppermute | solution.py:30
  226.2 2.3 collective-permute-done
  228.5 3.0 %while.24 = (s32[]{:T(128)}, f32[4,6,128]{2,1,0:T(8,128)S(1)}, f32[3,512]{1,0:T(4,128)S(1)}, f32[4,6,128]{2,1,0:T(8,128)S(1)}, f32[512]{0:T(512)S(1)}, /*index=5*/f32[3,512]{1,0:T(4,128)S(1)}, s32[]{:T(128)}) while((s32[]{:T(128)}, f32[4,6,128]{2,1,0:T(8,128)S(1)}, f32[3,512]{1,0:T(4,128)S(1)}, f32[4,6,128]{2,1,0:T(8,128)S(1)}, ...), condition=%wide.region_6.6_spmd, body=%wide.region_1.5_spmd.sunk | while | flops 3014658 | bytes 2153557 | solution.py:71
  235.4 4.2 %collective-permute-done.1 = f32[6,512]{1,0:T(8,128)S(1)} collective-permute-done((f32[6,512]{1,0:T(8,128)S(1)}, f32[6,512]{1,0:T(8,128)S(1)}, u32[]{:S(2)}, u32[]{:S(2)}) %collective-permute-start.1) | collective-permute-done | bytes 12320 | tf_op jit(solution)/shard_map/while/body/eval_jaxpr/ppermute | solution.py:30
  241.8 29.8 %all_to_all.10 = f32[32,6,16]{2,1,0:T(8,128)S(1)} all-to-all(f32[32,6,16]{2,1,0:T(8,128)S(1)} %copy.49), channel_id=1, replica_groups=mesh['blk'=16,'grp'=32] {'grp'}, dimensions={0} | all-to-all | bytes 24576 | tf_op jit(solution)/shard_map/all_to_all | solution.py:41
  (495 shorter events, 121.7 us)
Async XLA Ops:
  0.6 0.7 copy-start.3
  1.3 0.7 copy-start.2
  2.8 0.6 copy-start.1
  3.4 0.7 copy-start.4
  5.4 19.8 %all-to-all-start = ((f32[32,6,16]{2,1,0:T(8,128)}), f32[32,6,16]{2,1,0:T(8,128)S(1)}, u32[]{:S(2)}, u32[]{:S(2)}) async-start(f32[32,6,16]{2,1,0:T(8,128)} %broadcast_in_dim.37), calls=%async_computation | async-start | bytes 262144 | tf_op jit(solution)/shard_map/all_to_all | solution.py:19
  25.4 0.7 copy-start
  29.1 13.1 %collective-permute-start.1 = (f32[6,512]{1,0:T(8,128)S(1)}, f32[6,512]{1,0:T(8,128)S(1)}, u32[]{:S(2)}, u32[]{:S(2)}) collective-permute-start(f32[6,512]{1,0:T(8,128)S(1)} %bitcast_add_fusion.2), channel_id=1, source_target_pairs={{0,32},{32,64},{64,96},{96,128},{128,160},{160,192},{192,224},{224... | collective-permute-start | bytes 36872 | tf_op jit(solution)/shard_map/while/body/eval_jaxpr/ppermute | solution.py:30
  32.2 11.9 %collective-permute-start = (f32[6,512]{1,0:T(8,128)S(1)}, f32[6,512]{1,0:T(8,128)S(1)}, u32[]{:S(2)}, u32[]{:S(2)}) collective-permute-start(f32[6,512]{1,0:T(8,128)S(1)} %bitcast.28), channel_id=1, source_target_pairs={{0,32},{32,64},{64,96},{96,128},{128,160},{160,192},{192,224},{224... | collective-permute-start | bytes 36872 | tf_op jit(solution)/shard_map/while/body/eval_jaxpr/ppermute | solution.py:30
  47.2 8.1 %collective-permute-start.1 = (f32[6,512]{1,0:T(8,128)S(1)}, f32[6,512]{1,0:T(8,128)S(1)}, u32[]{:S(2)}, u32[]{:S(2)}) collective-permute-start(f32[6,512]{1,0:T(8,128)S(1)} %bitcast_add_fusion.2), channel_id=1, source_target_pairs={{0,32},{32,64},{64,96},{96,128},{128,160},{160,192},{192,224},{224... | collective-permute-start | bytes 36872 | tf_op jit(solution)/shard_map/while/body/eval_jaxpr/ppermute | solution.py:30
  49.1 8.3 %collective-permute-start = (f32[6,512]{1,0:T(8,128)S(1)}, f32[6,512]{1,0:T(8,128)S(1)}, u32[]{:S(2)}, u32[]{:S(2)}) collective-permute-start(f32[6,512]{1,0:T(8,128)S(1)} %bitcast.28), channel_id=1, source_target_pairs={{0,32},{32,64},{64,96},{96,128},{128,160},{160,192},{192,224},{224... | collective-permute-start | bytes 36872 | tf_op jit(solution)/shard_map/while/body/eval_jaxpr/ppermute | solution.py:30
  60.5 8.1 %collective-permute-start.1 = (f32[6,512]{1,0:T(8,128)S(1)}, f32[6,512]{1,0:T(8,128)S(1)}, u32[]{:S(2)}, u32[]{:S(2)}) collective-permute-start(f32[6,512]{1,0:T(8,128)S(1)} %bitcast_add_fusion.2), channel_id=1, source_target_pairs={{0,32},{32,64},{64,96},{96,128},{128,160},{160,192},{192,224},{224... | collective-permute-start | bytes 36872 | tf_op jit(solution)/shard_map/while/body/eval_jaxpr/ppermute | solution.py:30
  62.4 8.1 %collective-permute-start = (f32[6,512]{1,0:T(8,128)S(1)}, f32[6,512]{1,0:T(8,128)S(1)}, u32[]{:S(2)}, u32[]{:S(2)}) collective-permute-start(f32[6,512]{1,0:T(8,128)S(1)} %bitcast.28), channel_id=1, source_target_pairs={{0,32},{32,64},{64,96},{96,128},{128,160},{160,192},{192,224},{224... | collective-permute-start | bytes 36872 | tf_op jit(solution)/shard_map/while/body/eval_jaxpr/ppermute | solution.py:30
  73.6 8.1 %collective-permute-start.1 = (f32[6,512]{1,0:T(8,128)S(1)}, f32[6,512]{1,0:T(8,128)S(1)}, u32[]{:S(2)}, u32[]{:S(2)}) collective-permute-start(f32[6,512]{1,0:T(8,128)S(1)} %bitcast_add_fusion.2), channel_id=1, source_target_pairs={{0,32},{32,64},{64,96},{96,128},{128,160},{160,192},{192,224},{224... | collective-permute-start | bytes 36872 | tf_op jit(solution)/shard_map/while/body/eval_jaxpr/ppermute | solution.py:30
  75.5 8.1 %collective-permute-start = (f32[6,512]{1,0:T(8,128)S(1)}, f32[6,512]{1,0:T(8,128)S(1)}, u32[]{:S(2)}, u32[]{:S(2)}) collective-permute-start(f32[6,512]{1,0:T(8,128)S(1)} %bitcast.28), channel_id=1, source_target_pairs={{0,32},{32,64},{64,96},{96,128},{128,160},{160,192},{192,224},{224... | collective-permute-start | bytes 36872 | tf_op jit(solution)/shard_map/while/body/eval_jaxpr/ppermute | solution.py:30
  86.7 8.1 %collective-permute-start.1 = (f32[6,512]{1,0:T(8,128)S(1)}, f32[6,512]{1,0:T(8,128)S(1)}, u32[]{:S(2)}, u32[]{:S(2)}) collective-permute-start(f32[6,512]{1,0:T(8,128)S(1)} %bitcast_add_fusion.2), channel_id=1, source_target_pairs={{0,32},{32,64},{64,96},{96,128},{128,160},{160,192},{192,224},{224... | collective-permute-start | bytes 36872 | tf_op jit(solution)/shard_map/while/body/eval_jaxpr/ppermute | solution.py:30
  88.6 8.1 %collective-permute-start = (f32[6,512]{1,0:T(8,128)S(1)}, f32[6,512]{1,0:T(8,128)S(1)}, u32[]{:S(2)}, u32[]{:S(2)}) collective-permute-start(f32[6,512]{1,0:T(8,128)S(1)} %bitcast.28), channel_id=1, source_target_pairs={{0,32},{32,64},{64,96},{96,128},{128,160},{160,192},{192,224},{224... | collective-permute-start | bytes 36872 | tf_op jit(solution)/shard_map/while/body/eval_jaxpr/ppermute | solution.py:30
  99.7 8.1 %collective-permute-start.1 = (f32[6,512]{1,0:T(8,128)S(1)}, f32[6,512]{1,0:T(8,128)S(1)}, u32[]{:S(2)}, u32[]{:S(2)}) collective-permute-start(f32[6,512]{1,0:T(8,128)S(1)} %bitcast_add_fusion.2), channel_id=1, source_target_pairs={{0,32},{32,64},{64,96},{96,128},{128,160},{160,192},{192,224},{224... | collective-permute-start | bytes 36872 | tf_op jit(solution)/shard_map/while/body/eval_jaxpr/ppermute | solution.py:30
  101.7 8.1 %collective-permute-start = (f32[6,512]{1,0:T(8,128)S(1)}, f32[6,512]{1,0:T(8,128)S(1)}, u32[]{:S(2)}, u32[]{:S(2)}) collective-permute-start(f32[6,512]{1,0:T(8,128)S(1)} %bitcast.28), channel_id=1, source_target_pairs={{0,32},{32,64},{64,96},{96,128},{128,160},{160,192},{192,224},{224... | collective-permute-start | bytes 36872 | tf_op jit(solution)/shard_map/while/body/eval_jaxpr/ppermute | solution.py:30
  112.8 8.1 %collective-permute-start.1 = (f32[6,512]{1,0:T(8,128)S(1)}, f32[6,512]{1,0:T(8,128)S(1)}, u32[]{:S(2)}, u32[]{:S(2)}) collective-permute-start(f32[6,512]{1,0:T(8,128)S(1)} %bitcast_add_fusion.2), channel_id=1, source_target_pairs={{0,32},{32,64},{64,96},{96,128},{128,160},{160,192},{192,224},{224... | collective-permute-start | bytes 36872 | tf_op jit(solution)/shard_map/while/body/eval_jaxpr/ppermute | solution.py:30
  114.8 8.1 %collective-permute-start = (f32[6,512]{1,0:T(8,128)S(1)}, f32[6,512]{1,0:T(8,128)S(1)}, u32[]{:S(2)}, u32[]{:S(2)}) collective-permute-start(f32[6,512]{1,0:T(8,128)S(1)} %bitcast.28), channel_id=1, source_target_pairs={{0,32},{32,64},{64,96},{96,128},{128,160},{160,192},{192,224},{224... | collective-permute-start | bytes 36872 | tf_op jit(solution)/shard_map/while/body/eval_jaxpr/ppermute | solution.py:30
  125.9 8.1 %collective-permute-start.1 = (f32[6,512]{1,0:T(8,128)S(1)}, f32[6,512]{1,0:T(8,128)S(1)}, u32[]{:S(2)}, u32[]{:S(2)}) collective-permute-start(f32[6,512]{1,0:T(8,128)S(1)} %bitcast_add_fusion.2), channel_id=1, source_target_pairs={{0,32},{32,64},{64,96},{96,128},{128,160},{160,192},{192,224},{224... | collective-permute-start | bytes 36872 | tf_op jit(solution)/shard_map/while/body/eval_jaxpr/ppermute | solution.py:30
  127.9 8.1 %collective-permute-start = (f32[6,512]{1,0:T(8,128)S(1)}, f32[6,512]{1,0:T(8,128)S(1)}, u32[]{:S(2)}, u32[]{:S(2)}) collective-permute-start(f32[6,512]{1,0:T(8,128)S(1)} %bitcast.28), channel_id=1, source_target_pairs={{0,32},{32,64},{64,96},{96,128},{128,160},{160,192},{192,224},{224... | collective-permute-start | bytes 36872 | tf_op jit(solution)/shard_map/while/body/eval_jaxpr/ppermute | solution.py:30
  139.0 8.1 %collective-permute-start.1 = (f32[6,512]{1,0:T(8,128)S(1)}, f32[6,512]{1,0:T(8,128)S(1)}, u32[]{:S(2)}, u32[]{:S(2)}) collective-permute-start(f32[6,512]{1,0:T(8,128)S(1)} %bitcast_add_fusion.2), channel_id=1, source_target_pairs={{0,32},{32,64},{64,96},{96,128},{128,160},{160,192},{192,224},{224... | collective-permute-start | bytes 36872 | tf_op jit(solution)/shard_map/while/body/eval_jaxpr/ppermute | solution.py:30
  141.0 8.1 %collective-permute-start = (f32[6,512]{1,0:T(8,128)S(1)}, f32[6,512]{1,0:T(8,128)S(1)}, u32[]{:S(2)}, u32[]{:S(2)}) collective-permute-start(f32[6,512]{1,0:T(8,128)S(1)} %bitcast.28), channel_id=1, source_target_pairs={{0,32},{32,64},{64,96},{96,128},{128,160},{160,192},{192,224},{224... | collective-permute-start | bytes 36872 | tf_op jit(solution)/shard_map/while/body/eval_jaxpr/ppermute | solution.py:30
  152.1 8.1 %collective-permute-start.1 = (f32[6,512]{1,0:T(8,128)S(1)}, f32[6,512]{1,0:T(8,128)S(1)}, u32[]{:S(2)}, u32[]{:S(2)}) collective-permute-start(f32[6,512]{1,0:T(8,128)S(1)} %bitcast_add_fusion.2), channel_id=1, source_target_pairs={{0,32},{32,64},{64,96},{96,128},{128,160},{160,192},{192,224},{224... | collective-permute-start | bytes 36872 | tf_op jit(solution)/shard_map/while/body/eval_jaxpr/ppermute | solution.py:30
  154.1 8.1 %collective-permute-start = (f32[6,512]{1,0:T(8,128)S(1)}, f32[6,512]{1,0:T(8,128)S(1)}, u32[]{:S(2)}, u32[]{:S(2)}) collective-permute-start(f32[6,512]{1,0:T(8,128)S(1)} %bitcast.28), channel_id=1, source_target_pairs={{0,32},{32,64},{64,96},{96,128},{128,160},{160,192},{192,224},{224... | collective-permute-start | bytes 36872 | tf_op jit(solution)/shard_map/while/body/eval_jaxpr/ppermute | solution.py:30
  165.2 8.1 %collective-permute-start.1 = (f32[6,512]{1,0:T(8,128)S(1)}, f32[6,512]{1,0:T(8,128)S(1)}, u32[]{:S(2)}, u32[]{:S(2)}) collective-permute-start(f32[6,512]{1,0:T(8,128)S(1)} %bitcast_add_fusion.2), channel_id=1, source_target_pairs={{0,32},{32,64},{64,96},{96,128},{128,160},{160,192},{192,224},{224... | collective-permute-start | bytes 36872 | tf_op jit(solution)/shard_map/while/body/eval_jaxpr/ppermute | solution.py:30
  167.2 8.1 %collective-permute-start = (f32[6,512]{1,0:T(8,128)S(1)}, f32[6,512]{1,0:T(8,128)S(1)}, u32[]{:S(2)}, u32[]{:S(2)}) collective-permute-start(f32[6,512]{1,0:T(8,128)S(1)} %bitcast.28), channel_id=1, source_target_pairs={{0,32},{32,64},{64,96},{96,128},{128,160},{160,192},{192,224},{224... | collective-permute-start | bytes 36872 | tf_op jit(solution)/shard_map/while/body/eval_jaxpr/ppermute | solution.py:30
  178.3 8.1 %collective-permute-start.1 = (f32[6,512]{1,0:T(8,128)S(1)}, f32[6,512]{1,0:T(8,128)S(1)}, u32[]{:S(2)}, u32[]{:S(2)}) collective-permute-start(f32[6,512]{1,0:T(8,128)S(1)} %bitcast_add_fusion.2), channel_id=1, source_target_pairs={{0,32},{32,64},{64,96},{96,128},{128,160},{160,192},{192,224},{224... | collective-permute-start | bytes 36872 | tf_op jit(solution)/shard_map/while/body/eval_jaxpr/ppermute | solution.py:30
  180.3 8.1 %collective-permute-start = (f32[6,512]{1,0:T(8,128)S(1)}, f32[6,512]{1,0:T(8,128)S(1)}, u32[]{:S(2)}, u32[]{:S(2)}) collective-permute-start(f32[6,512]{1,0:T(8,128)S(1)} %bitcast.28), channel_id=1, source_target_pairs={{0,32},{32,64},{64,96},{96,128},{128,160},{160,192},{192,224},{224... | collective-permute-start | bytes 36872 | tf_op jit(solution)/shard_map/while/body/eval_jaxpr/ppermute | solution.py:30
  191.4 8.6 %collective-permute-start.1 = (f32[6,512]{1,0:T(8,128)S(1)}, f32[6,512]{1,0:T(8,128)S(1)}, u32[]{:S(2)}, u32[]{:S(2)}) collective-permute-start(f32[6,512]{1,0:T(8,128)S(1)} %bitcast_add_fusion.2), channel_id=1, source_target_pairs={{0,32},{32,64},{64,96},{96,128},{128,160},{160,192},{192,224},{224... | collective-permute-start | bytes 36872 | tf_op jit(solution)/shard_map/while/body/eval_jaxpr/ppermute | solution.py:30
  193.4 8.6 %collective-permute-start = (f32[6,512]{1,0:T(8,128)S(1)}, f32[6,512]{1,0:T(8,128)S(1)}, u32[]{:S(2)}, u32[]{:S(2)}) collective-permute-start(f32[6,512]{1,0:T(8,128)S(1)} %bitcast.28), channel_id=1, source_target_pairs={{0,32},{32,64},{64,96},{96,128},{128,160},{160,192},{192,224},{224... | collective-permute-start | bytes 36872 | tf_op jit(solution)/shard_map/while/body/eval_jaxpr/ppermute | solution.py:30
  205.0 8.1 %collective-permute-start.1 = (f32[6,512]{1,0:T(8,128)S(1)}, f32[6,512]{1,0:T(8,128)S(1)}, u32[]{:S(2)}, u32[]{:S(2)}) collective-permute-start(f32[6,512]{1,0:T(8,128)S(1)} %bitcast_add_fusion.2), channel_id=1, source_target_pairs={{0,32},{32,64},{64,96},{96,128},{128,160},{160,192},{192,224},{224... | collective-permute-start | bytes 36872 | tf_op jit(solution)/shard_map/while/body/eval_jaxpr/ppermute | solution.py:30
  206.9 8.1 %collective-permute-start = (f32[6,512]{1,0:T(8,128)S(1)}, f32[6,512]{1,0:T(8,128)S(1)}, u32[]{:S(2)}, u32[]{:S(2)}) collective-permute-start(f32[6,512]{1,0:T(8,128)S(1)} %bitcast.28), channel_id=1, source_target_pairs={{0,32},{32,64},{64,96},{96,128},{128,160},{160,192},{192,224},{224... | collective-permute-start | bytes 36872 | tf_op jit(solution)/shard_map/while/body/eval_jaxpr/ppermute | solution.py:30
  218.1 8.1 %collective-permute-start.1 = (f32[6,512]{1,0:T(8,128)S(1)}, f32[6,512]{1,0:T(8,128)S(1)}, u32[]{:S(2)}, u32[]{:S(2)}) collective-permute-start(f32[6,512]{1,0:T(8,128)S(1)} %bitcast_add_fusion.2), channel_id=1, source_target_pairs={{0,32},{32,64},{64,96},{96,128},{128,160},{160,192},{192,224},{224... | collective-permute-start | bytes 36872 | tf_op jit(solution)/shard_map/while/body/eval_jaxpr/ppermute | solution.py:30
  220.0 8.5 %collective-permute-start = (f32[6,512]{1,0:T(8,128)S(1)}, f32[6,512]{1,0:T(8,128)S(1)}, u32[]{:S(2)}, u32[]{:S(2)}) collective-permute-start(f32[6,512]{1,0:T(8,128)S(1)} %bitcast.28), channel_id=1, source_target_pairs={{0,32},{32,64},{64,96},{96,128},{128,160},{160,192},{192,224},{224... | collective-permute-start | bytes 36872 | tf_op jit(solution)/shard_map/while/body/eval_jaxpr/ppermute | solution.py:30
  231.6 8.1 %collective-permute-start.1 = (f32[6,512]{1,0:T(8,128)S(1)}, f32[6,512]{1,0:T(8,128)S(1)}, u32[]{:S(2)}, u32[]{:S(2)}) collective-permute-start(f32[6,512]{1,0:T(8,128)S(1)} %bitcast_add_fusion.2), channel_id=1, source_target_pairs={{0,32},{32,64},{64,96},{96,128},{128,160},{160,192},{192,224},{224... | collective-permute-start | bytes 36872 | tf_op jit(solution)/shard_map/while/body/eval_jaxpr/ppermute | solution.py:30
  233.5 8.1 %collective-permute-start = (f32[6,512]{1,0:T(8,128)S(1)}, f32[6,512]{1,0:T(8,128)S(1)}, u32[]{:S(2)}, u32[]{:S(2)}) collective-permute-start(f32[6,512]{1,0:T(8,128)S(1)} %bitcast.28), channel_id=1, source_target_pairs={{0,32},{32,64},{64,96},{96,128},{128,160},{160,192},{192,224},{224... | collective-permute-start | bytes 36872 | tf_op jit(solution)/shard_map/while/body/eval_jaxpr/ppermute | solution.py:30
where the time goes:
time: 273 us; the launch traced here: 272 us
  waiting for transfers between devices  111 us (41%)
  starting transfers between devices  75.1 us (28%)
  other arithmetic  47 us (17%)
  blocking collectives  29.8 us (11%)
  local copies, waits for them, and re-layouts  5.56 us (2%)
  loops' own time  3.26 us (1%)
    ppermute x32, waiting for transfers between devices, from_behind(): lax.ppermute(shard, axis, [(i, (i + by) % count) for i in range(count)])  101 us
    ppermute x32, starting transfers between devices, from_behind(): lax.ppermute(shard, axis, [(i, (i + by) % count) for i in range(count)])  64.7 us
    all_to_all x1, blocking collectives, sent_and_summed(): lax.all_to_all(parts, axis, split_axis=0, concat_axis=0, tiled=True)  29.8 us
    reduce_sum x64, other arithmetic, one_block(): accel_part = jnp.sum(weight[None] * separation, 2)  25.6 us
    reduce_sum x64, other arithmetic, one_block(): distance = jnp.sum(separation * separation, 0) + SOFTENING  13.8 us
    all_to_all x1, starting transfers between devices, copy_for_each(): lax.all_to_all(jnp.broadcast_to(shard[None], (count, *shard.shape)), axis...  10.3 us
    all_to_all x1, waiting for transfers between devices, copy_for_each(): lax.all_to_all(jnp.broadcast_to(shard[None], (count, *shard.shape)), axis...  9.43 us
  transfers between devices with their start and end apart: 33, of which 33 were waited for; matrix products, arithmetic and copies ran while one was open for 0% of the time, Pallas kernels for 0%

commit v1 on v0

v1 whole, which is shorter than its diff:
```python
import jax
import jax.numpy as jnp
from jax import lax
from jax.experimental import pallas as pl
from jax.experimental.pallas import tpu as pltpu
from jax.sharding import PartitionSpec as P

SOFTENING = 0.0001


def prologue_kernel(offsets, position, velocity, accel_old, jerk_old, mass, elapsed, predicted, sources, targets):
    step_row = elapsed[...]
    half = step_row * step_row * 0.5
    sixth = half * step_row * (1.0 / 3.0)
    new_position = position[...] + step_row * velocity[...] + half * accel_old[...] + sixth * jerk_old[...]
    new_velocity = velocity[...] + step_row * accel_old[...] + half * jerk_old[...]
    predicted[0:3, :] = new_position
    predicted[3:6, :] = new_velocity
    everything = jnp.concatenate([new_position, new_velocity, mass[...], mass[...]], 0)
    for copy in range(sources.shape[0]):
        sources[copy] = everything
    active, stars = targets.shape[1], position.shape[1]
    columns = lax.broadcasted_iota(jnp.int32, (active, stars), 1)
    chosen = columns == offsets[...]
    picked = []
    for row in range(6):
        values = jnp.broadcast_to(everything[row : row + 1], (active, stars))
        picked.append(jnp.sum(jnp.where(chosen, values, 0.0), 1, keepdims=True))
    stacked = jnp.concatenate(picked + picked[:2], 1)
    for copy in range(targets.shape[0]):
        targets[copy] = stacked


def interact_kernel(sources, targets, result):
    count, stars = sources.shape[1], sources.shape[2]
    rows = 8

    def one_group(group, unused):
        start = pl.multiple_of(group * rows, rows)
        here = targets[pl.ds(start, rows), :]
        own = [jnp.broadcast_to(here[:, k : k + 1], (rows, 128)) for k in range(6)]

        def one_chunk(chunk, carry):
            sums = list(carry)
            for part in range(stars // 128):
                there = [
                    jnp.broadcast_to(sources[chunk, k : k + 1, part * 128 : part * 128 + 128], (rows, 128))
                    for k in range(7)
                ]
                r = [there[k] - own[k] for k in range(3)]
                u = [there[k + 3] - own[k + 3] for k in range(3)]
                q = r[0] * r[0] + r[1] * r[1] + r[2] * r[2] + SOFTENING
                s = r[0] * u[0] + r[1] * u[1] + r[2] * u[2]
                inverse = lax.rsqrt(q)
                squared = inverse * inverse
                weight = there[6] * inverse * squared
                radial = s * squared
                for k in range(3):
                    pull = weight * r[k]
                    sums[k] = sums[k] + pull
                    sums[k + 3] = sums[k + 3] + weight * u[k]
                    sums[k + 6] = sums[k + 6] + radial * pull
            return tuple(sums)

        zero = jnp.zeros((rows, 128), jnp.float32)
        sums = lax.fori_loop(0, sources.shape[0], one_chunk, (zero,) * 9)
        accel = [jnp.sum(sums[k], 1, keepdims=True) for k in range(3)]
        jerk = [jnp.sum(sums[k + 3] - 3.0 * sums[k + 6], 1, keepdims=True) for k in range(3)]
        result[pl.ds(start, rows), :] = jnp.concatenate(accel + jerk + accel[:2], 1)
        return unused

    lax.fori_loop(0, targets.shape[0] // rows, one_group, 0)


def local(position, velocity, accel_old, jerk_old, mass, elapsed, active_index):
    stars, active = position.shape[1], active_index.shape[0]
    blocks, members = lax.axis_size("blk"), lax.axis_size("grp")
    device = lax.axis_index("blk") * members + lax.axis_index("grp")
    offsets = active_index - device * stars
    f32 = jnp.float32
    predicted, sources, targets = pl.pallas_call(
        prologue_kernel,
        out_shape=(
            jax.ShapeDtypeStruct((6, stars), f32),
            jax.ShapeDtypeStruct((blocks, 8, stars), f32),
            jax.ShapeDtypeStruct((members, active, 8), f32),
        ),
        name="prologue",
    )(offsets[:, None], position, velocity, accel_old, jerk_old, mass[None], elapsed[None])
    targets = lax.all_to_all(targets, "grp", 0, 0, tiled=True)
    sources = lax.all_to_all(sources, "blk", 0, 0, tiled=True)
    result = pl.pallas_call(
        interact_kernel,
        out_shape=jax.ShapeDtypeStruct((members * active, 8), f32),
        name="interact",
    )(sources, targets.reshape(members * active, 8))
    parts = lax.all_to_all(result.reshape(members, active, 8), "grp", 0, 0, tiled=True)
    owned = parts.sum(axis=0).T
    return (predicted, owned[0:3], owned[3:6])


def solution(mesh):
    whole = P(None, ("blk", "grp"))
    flat = P(("blk", "grp"))
    return jax.shard_map(
        local,
        mesh=mesh,
        in_specs=(whole, whole, whole, whole, flat, flat, flat),
        out_specs=(whole, whole, whole),
        check_vma=False,
    )
```

time: 273 us -> 102 us (0.37)
  waiting for transfers between devices: 111 us -> 8.15 us
  starting transfers between devices: 75.1 us -> 12.2 us
  other arithmetic: 47 us -> 1.41 us
  Pallas kernels: 0 us -> 40.9 us
  loops' own time: 3.26 us -> 0 us
    ppermute x32 -> x0, waiting for transfers between devices: 101 us -> none  [from_behind(): lax.ppermute(shard, axis, [(i, (i + by) % count) for i in range(count)])]
    ppermute x32 -> x0, starting transfers between devices: 64.7 us -> none  [from_behind(): lax.ppermute(shard, axis, [(i, (i + by) % count) for i in range(count)])]
    pallas_call x0 -> x2, Pallas kernels: none -> 40.9 us  [the longest x1 39.3 us: local(): pl.pallas_call(interact_kernel, out_shape=jax.ShapeDtypeStruct((members *...]
    reduce_sum x129 -> x1, other arithmetic: 39.5 us -> 0.04 us  [local(): owned = parts.sum(axis=0).T]
    div x64 -> x0, other arithmetic: 5.19 us -> none  [one_block(): radial = 3.0 * jnp.sum(separation * relative, 0) / distance]
    another operation x17 -> x0, loops' own time: 3.26 us -> none  [the longest x16 2.66 us: interact(): result = lax.map(one_block, stacked)]
    all_to_all x1 -> x2, blocking collectives: 29.8 us -> 30.4 us  [the longest x1 17.5 us: local(): targets = lax.all_to_all(targets, 'grp', 0, 0, tiled=True)]
  transfers between devices with their start and end apart: 33 -> 1, of which waited for: 33 -> 1; matrix products, arithmetic and copies ran while one was open for 0% -> 2% of each run, Pallas kernels for 0% -> 0%
where the time goes in v1:
time: 102 us; the launch traced here: 101 us
  Pallas kernels  40.9 us (40%)
  blocking collectives  30.4 us (30%)
  starting transfers between devices  12.2 us (12%)
  waiting for transfers between devices  8.15 us (8%)
  local copies, waits for them, and re-layouts  7.36 us (7%)
  other arithmetic  1.41 us (1%)
    pallas_call x1, Pallas kernels, local(): pl.pallas_call(interact_kernel, out_shape=jax.ShapeDtypeStruct((members *...  39.3 us
    all_to_all x1, blocking collectives, local(): targets = lax.all_to_all(targets, 'grp', 0, 0, tiled=True)  17.5 us
    all_to_all x1, blocking collectives, local(): lax.all_to_all(result.reshape(members, active, 8), 'grp', 0, 0, tiled=True)  12.9 us
    all_to_all x1, starting transfers between devices, local(): sources = lax.all_to_all(sources, 'blk', 0, 0, tiled=True)  12.2 us
    all_to_all x1, waiting for transfers between devices, local(): sources = lax.all_to_all(sources, 'blk', 0, 0, tiled=True)  8.15 us
    unnamed x11, local copies, waits for them, and re-layouts  3.16 us
  transfers between devices with their start and end apart: 1, of which 1 were waited for; matrix products, arithmetic and copies ran while one was open for 2% of the time, Pallas kernels for 0%

profile of v1, /device:TPU:1, one launch (start us, length us, event | category | flops | bytes accessed | tf_op | source)
XLA Modules:
  0.0 101.2 jit_solution(437039194033853334)
XLA Ops:
  0.6 0.0 copy-start.1
  0.6 0.6 copy-done.1
  1.3 0.7 copy.11.offsets
  2.0 1.7 %prologue.1 = (f32[6,512]{1,0:T(8,128)}, f32[16,8,512]{2,1,0:T(8,128)}, f32[32,16,8]{2,1,0:T(8,128)}) custom-call(s32[16,1]{1,0:T(8,128)} %copy.11.offsets, f32[3,512]{1,0:T(4,128)} %position.1, f32[3,512]{1,0:T(4,128)} %velocity.1, f32[3,512]{1,0:T(4,128)} %accel_old.1, f32[3,512]{1,0:T(4,128)} %jerk_old.1, f32[1,512]{1,0:T(1,128)} %bitcast.18, ...), custom_call_target="tpu_custom_call" | custom-call | tf_op jit(solution)/shard_map/prologue/pallas_call | solution.py:81
  3.6 1.1 %copy.12 = f32[32,16,8]{1,2,0:T(8,128)S(1)} copy(f32[32,16,8]{2,1,0:T(8,128)} %get-tuple-element.8) | data formatting | bytes 32768 | tf_op jit(solution)/shard_map/prologue/pallas_call | solution.py:81
  4.7 0.1 reshape.14
  4.8 17.5 %all_to_all.15 = f32[32,1,128]{2,1,0:T(1,128)S(1)} all-to-all(f32[32,1,128]{2,1,0:T(1,128)S(1)} %reshape.14), channel_id=1, replica_groups=mesh['blk'=16,'grp'=32] {'grp'}, dimensions={0} | all-to-all | bytes 32768 | tf_op jit(solution)/shard_map/all_to_all | solution.py:90
  22.3 12.2 %all-to-all-start = ((f32[16,8,512]{2,1,0:T(8,128)}), f32[16,8,512]{2,1,0:T(8,128)S(1)}, u32[]{:S(2)}, u32[]{:S(2)}) async-start(f32[16,8,512]{2,1,0:T(8,128)} %get-tuple-element.7), calls=%async_computation | async-start | bytes 524288 | tf_op jit(solution)/shard_map/all_to_all | solution.py:91
  34.5 0.5 broadcast
  35.0 0.7 reduce
  35.7 0.1 reshape.15
  35.8 0.8 copy.13
  36.6 8.1 %all-to-all-done.sources = f32[16,8,512]{2,1,0:T(8,128)S(1)} async-done(((f32[16,8,512]{2,1,0:T(8,128)}), f32[16,8,512]{2,1,0:T(8,128)S(1)}, u32[]{:S(2)}, u32[]{:S(2)}) %all-to-all-start) | async-done | bytes 262176 | tf_op jit(solution)/shard_map/all_to_all | solution.py:91
  44.8 0.0 copy-start
  44.8 0.7 copy-done
  45.5 39.3 %interact.1 = f32[512,8]{1,0:T(8,128)} custom-call(f32[16,8,512]{2,1,0:T(8,128)} %copy-done, f32[512,8]{1,0:T(8,128)} %bitcast.12), custom_call_target="tpu_custom_call" | custom-call | tf_op jit(solution)/shard_map/interact/pallas_call | solution.py:92
  84.7 1.1 %copy.14 = f32[32,16,8]{1,2,0:T(8,128)S(1)} copy(f32[32,16,8]{2,1,0:T(8,128)} %bitcast.13) | data formatting | bytes 32768 | tf_op jit(solution)/shard_map/reshape | solution.py:97
  85.8 0.1 reshape.16
  85.9 12.9 %all_to_all.16 = f32[32,1,128]{2,1,0:T(1,128)S(1)} all-to-all(f32[32,1,128]{2,1,0:T(1,128)S(1)} %reshape.16), channel_id=1, replica_groups=mesh['blk'=16,'grp'=32] {'grp'}, dimensions={0} | all-to-all | bytes 32768 | tf_op jit(solution)/shard_map/all_to_all | solution.py:97
  98.9 0.7 reduce.1
  99.6 0.1 reshape.17
  99.7 0.1 copy.18
  99.8 0.1 fusion
  99.8 0.7 copy.16
  100.5 0.7 copy.17
  (2 shorter events, 0.0 us)
Async XLA Ops:
  0.6 0.7 copy-start.1
  22.3 22.5 %all-to-all-start = ((f32[16,8,512]{2,1,0:T(8,128)}), f32[16,8,512]{2,1,0:T(8,128)S(1)}, u32[]{:S(2)}, u32[]{:S(2)}) async-start(f32[16,8,512]{2,1,0:T(8,128)} %get-tuple-element.7), calls=%async_computation | async-start | bytes 524288 | tf_op jit(solution)/shard_map/all_to_all | solution.py:91
  44.8 0.7 copy-start

commit v2 on v1

v2 whole, which is shorter than its diff:
```python
import jax
import jax.numpy as jnp
from jax import lax
from jax.experimental import pallas as pl
from jax.experimental.pallas import tpu as pltpu
from jax.sharding import PartitionSpec as P

SOFTENING = 0.0001
LANES = 128
STEP = 256
F32 = jnp.float32
BF16 = jnp.bfloat16


def in_three(value):
    high = value.astype(BF16)
    rest = value - high.astype(F32)
    middle = rest.astype(BF16)
    low = (rest - middle.astype(F32)).astype(BF16)
    return high, middle, low


def lane_iota(shape):
    return lax.broadcasted_iota(jnp.int32, shape, len(shape) - 1)


def row_iota(shape):
    return lax.broadcasted_iota(jnp.int32, shape, 0)


def prologue_kernel(first, active_index, position, velocity, accel_old, jerk_old, mass, elapsed, predicted, sources, targets):
    active, stars = active_index.shape[1], position.shape[1]
    step_row = elapsed[...]
    half = step_row * step_row * 0.5
    sixth = half * step_row * (1.0 / 3.0)
    new_position = position[...] + step_row * velocity[...] + half * accel_old[...] + sixth * jerk_old[...]
    new_velocity = velocity[...] + step_row * accel_old[...] + half * jerk_old[...]
    predicted[0:3, :] = new_position
    predicted[3:6, :] = new_velocity
    everything = jnp.concatenate([new_position, new_velocity, mass[...], jnp.ones_like(step_row)], 0)
    for copy in range(sources.shape[0]):
        sources[copy] = everything
    offsets = active_index[...] - first[0]
    chosen = jnp.where(row_iota((stars, active)) == offsets, 1.0, 0.0).astype(BF16)
    high, middle, low = in_three(everything)
    dot = lambda piece: jnp.dot(piece, chosen, preferred_element_type=F32)
    picked = (dot(high) + dot(middle)) + dot(low)
    picked = jnp.concatenate([picked, jnp.zeros((8, LANES - active), F32)], 1)
    spread = pltpu.roll(picked, 0, 1, stride=active, stride_axis=0)
    line = jnp.sum(spread, 0, keepdims=True)
    targets[...] = jnp.broadcast_to(line, targets.shape)


def unpack_targets(message, active):
    rows = []
    for k in range(6):
        pieces = []
        for group in range(message.shape[0] // 8):
            part = message[group * 8 : group * 8 + 8, :]
            turned = pltpu.roll(part, (LANES - k * active) % LANES, 1) if k else part
            turned = pltpu.roll(turned, 0, 1, stride=active, stride_axis=0)
            kept = jnp.where(lane_iota((8, LANES)) // active == row_iota((8, LANES)), turned, 0.0)
            pieces.append(jnp.sum(kept, 0, keepdims=True))
        rows.append(jnp.concatenate(pieces, 1))
    return rows


def pack_results(rows, active, result):
    stacked = jnp.concatenate(rows + rows[:2], 0)
    piece, row = lane_iota((8, LANES)) // active, row_iota((8, LANES))
    for group in range(result.shape[0] // 8):
        part = stacked[:, group * LANES : group * LANES + LANES]
        total = jnp.zeros((8, LANES), F32)
        for shift in range(8):
            turned = pltpu.roll(part, shift * active, 1) if shift else part
            line = jnp.sum(jnp.where(piece == row, turned, 0.0), 0, keepdims=True)
            total = jnp.where((piece - row) % 8 == shift, jnp.broadcast_to(line, (8, LANES)), total)
        result[group * 8 : group * 8 + 8, :] = total


def radial_features(state, first_order):
    row = row_iota(state.shape)
    grid = jnp.where(row < 3, 1.5 * 2.0**20, 1.5 * 2.0**14)
    coarse = (state + grid) - grid
    fine = state - coarse
    exact = lambda value: value.astype(BF16).astype(F32)
    top = exact(coarse)
    bottom = coarse - top
    first = exact(fine)
    second = exact(fine - first)
    third = fine - first - second
    line = lambda value, k: value[k : k + 1]
    both = [line(coarse, k) * line(coarse, k + 3) for k in range(3)]
    whole = both[0] + both[1] + both[2]
    mixed = [line(coarse, k) * line(fine, k + 3) + line(fine, k) * line(state, k + 3) for k in range(3)]
    part = mixed[0] + mixed[1] + mixed[2]
    pieces = []
    for value in (whole, part):
        high = exact(value)
        middle = exact(value - high)
        pieces.append((high, middle, value - high - middle))
    pick = lambda upper, lower: jnp.where(row < 3, upper, lower)
    zero = jnp.zeros_like(state)
    groups = [
        (top, pieces[0][0]),
        (pick(top, bottom), pieces[0][1]),
        (zero, pieces[0][2]),
        (pick(top, first), pieces[1][0]),
        (pick(top, second), pieces[1][1]),
        (pick(first, top), pieces[1][2]),
        (pick(first, bottom), None),
        (first, None),
        (pick(second, top), None),
        (pick(second, bottom), None),
        (pick(third, top), None),
    ]
    rows = []
    for value, extra in groups:
        if not first_order:
            value = -jnp.concatenate([value[3:6], value[0:3], value[6:8]], 0)
        if extra is None:
            value = jnp.where(row < 6, value, 0.0)
        else:
            wide = jnp.broadcast_to(extra, value.shape)
            value = jnp.where(row < 6, value, jnp.where(row == (6 if first_order else 7), wide, 1.0))
        rows.append(value)
    rows += [zero] * (16 - len(rows))
    return jnp.concatenate(rows, 0)


def spread_columns(block, spread, count):
    columns = block.T
    for row in range(0, columns.shape[0], 8):
        for k in range(count):
            spread[k, row : row + 8, :] = jnp.broadcast_to(columns[row : row + 8, k : k + 1], (8, LANES))


def own_kernel(sources, message, result, spread, *, active):
    stars = sources.shape[1]
    spread_columns(sources[...], spread, 7)
    lines = unpack_targets(message[...], active)
    wide = message.shape[0] * active
    total = []
    for group in range(wide // LANES):
        own = [jnp.broadcast_to(line[:, group * LANES : group * LANES + LANES], (8, LANES)) for line in lines]

        def one(step, carry):
            sums = list(carry)
            for part in range(4):
                start = pl.multiple_of(step * 32, 32) + part * 8
                there = [spread[k, pl.ds(start, 8), :] for k in range(7)]
                r = [there[k] - own[k] for k in range(3)]
                u = [there[k + 3] - own[k + 3] for k in range(3)]
                q = r[0] * r[0] + r[1] * r[1] + r[2] * r[2] + SOFTENING
                s = r[0] * u[0] + r[1] * u[1] + r[2] * u[2]
                inverse = lax.rsqrt(q)
                squared = inverse * inverse
                weight = there[6] * inverse * squared
                radial = s * squared
                for k in range(3):
                    pull = weight * r[k]
                    sums[k] = sums[k] + pull
                    sums[k + 3] = sums[k + 3] + weight * u[k]
                    sums[k + 6] = sums[k + 6] + radial * pull
            return tuple(sums)

        sums = lax.fori_loop(0, stars // 32, one, (jnp.zeros((8, LANES), F32),) * 9)
        ready = list(sums[:3]) + [sums[k + 3] - 3.0 * sums[k + 6] for k in range(3)]
        total.append([jnp.sum(value, 0, keepdims=True) for value in ready])
    rows = [jnp.concatenate([part[k] for part in total], 1) for k in range(6)]
    result[...] = jnp.concatenate(rows + rows[:2], 0)


def main_kernel(block, sources, message, own_result, result, spread, target_rows, target_side, sum_w, sum_d, *, active):
    blocks, stars = sources.shape[0], sources.shape[2]
    wide = message.shape[0] * active
    groups = wide // LANES
    lines = unpack_targets(message[...], active)
    target_side[...] = radial_features(jnp.concatenate(lines + lines[:2], 0), False).astype(BF16)
    middle_of = lambda line: 0.5 * (jnp.min(line, 1, keepdims=True) + jnp.max(line, 1, keepdims=True))
    centers = [middle_of(line) for line in lines]
    center = jnp.concatenate(centers + [jnp.zeros((2, 1), F32)], 0)
    for k, row in enumerate(lines):
        for g in range(groups):
            target_rows[g, k * 8 : k * 8 + 8, :] = jnp.broadcast_to(row[:, g * LANES : g * LANES + LANES], (8, LANES))
    sum_w[...] = jnp.zeros(sum_w.shape, F32)
    sum_d[...] = jnp.zeros(sum_d.shape, F32)

    def one_block(turn, unused):
        chunk = lax.rem(block[0] + 1 + turn, blocks)
        here = sources[chunk]
        scaled = (here - center) * here[6:7]
        high, middle, low = in_three(scaled)
        stacked = jnp.concatenate([high.astype(F32), middle.astype(F32), low.astype(F32), jnp.zeros_like(scaled)], 0).astype(BF16)
        source_side = radial_features(here, True).T.astype(BF16)
        for step in range(stars // STEP):
            spread_columns(here[:, step * STEP : step * STEP + STEP], spread.at[step], 3)
            part = stacked[:, step * STEP : step * STEP + STEP]
            left = jnp.concatenate([part, part], 1)
            for half in range(groups // 2):
                lanes = slice(half * 2 * LANES, half * 2 * LANES + 2 * LANES)
                products = jnp.dot(
                    source_side[step * STEP : step * STEP + STEP], target_side[:, lanes], preferred_element_type=F32
                )
                full = [[], [], [], []]
                for row in range(0, STEP, 16):
                    across = [[], [], [], []]
                    for g in (2 * half, 2 * half + 1):
                        own = [target_rows[g, k * 8 : k * 8 + 8, :] for k in range(3)]
                        at_lane = (g - 2 * half) * LANES
                        both_w, both_d = [], []
                        for sub in range(2):
                            top = row + sub * 8
                            there = [spread[step, k, top : top + 8, :] for k in range(3)]
                            r = [there[k] - own[k] for k in range(3)]
                            q = r[0] * r[0] + r[1] * r[1] + (r[2] * r[2] + SOFTENING)
                            s = products[top : top + 8, at_lane : at_lane + LANES]
                            inverse = lax.rsqrt(q)
                            squared = inverse * inverse
                            weight = inverse * squared
                            both_w.append(weight)
                            both_d.append(weight * (s * squared))
                        for at, both in ((0, both_w), (2, both_d)):
                            value = jnp.concatenate(both, 0)
                            upper = value.astype(BF16)
                            across[at].append(upper)
                            across[at + 1].append((value - upper.astype(F32)).astype(BF16))
                    for at in range(4):
                        full[at].append(jnp.concatenate(across[at], 1))
                right_w = jnp.concatenate(full[0] + full[1], 0)
                right_d = jnp.concatenate(full[2] + full[3], 0)
                sum_w[:, lanes] += jnp.dot(left, right_w, preferred_element_type=F32)
                sum_d[:, lanes] += jnp.dot(left, right_d, preferred_element_type=F32)
        return unused

    lax.fori_loop(0, blocks - 1, one_block, 0)
    total_w = sum_w[0:8] + (sum_w[8:16] + sum_w[16:24])
    total_d = sum_d[0:8] + (sum_d[8:16] + sum_d[16:24])
    here = [jnp.concatenate([target_rows[g, k * 8 : k * 8 + 1, :] for g in range(groups)], 1) for k in range(6)]
    here = [value - middle for value, middle in zip(here, centers)]
    rows = []
    for k in range(3):
        rows.append(own_result[k : k + 1] + (total_w[k : k + 1] - here[k] * total_w[7:8]))
    for k in range(3):
        straight = total_w[k + 3 : k + 4] - here[k + 3] * total_w[7:8]
        inward = total_d[k : k + 1] - here[k] * total_d[7:8]
        rows.append(own_result[k + 3 : k + 4] + (straight - 3.0 * inward))
    pack_results(rows, active, result)


def final_kernel(parts, accel, jerk, *, active):
    line = jnp.broadcast_to(jnp.sum(parts[...], 0, keepdims=True), (8, LANES))
    for k in range(6):
        turned = pltpu.roll(line, LANES - k * active, 1) if k else line
        (accel if k < 3 else jerk)[k % 3 : k % 3 + 1, :] = turned[k : k + 1, :active]


def shape(*lengths):
    return jax.ShapeDtypeStruct(lengths, F32)


def local(position, velocity, accel_old, jerk_old, mass, elapsed, active_index):
    stars, active = position.shape[1], active_index.shape[0]
    blocks, members = lax.axis_size("blk"), lax.axis_size("grp")
    block = lax.axis_index("blk")
    first = ((block * members + lax.axis_index("grp")) * stars)[None]
    scalar = pl.BlockSpec(memory_space=pltpu.SMEM)
    vector = pl.BlockSpec(memory_space=pltpu.VMEM)
    predicted, sources, targets = pl.pallas_call(
        prologue_kernel,
        out_shape=(shape(6, stars), shape(blocks, 8, stars), shape(members, LANES)),
        in_specs=[scalar] + [vector] * 7,
        name="prologue",
    )(first, active_index[None], position, velocity, accel_old, jerk_old, mass[None], elapsed[None])
    message = lax.all_to_all(targets, "grp", 0, 0, tiled=True)
    gathered = lax.all_to_all(sources, "blk", 0, 0, tiled=True)
    result = interact(block[None], sources[0], gathered, message, active)
    parts = lax.all_to_all(result, "grp", 0, 0, tiled=True)
    accel, jerk = pl.pallas_call(
        lambda *refs: final_kernel(*refs, active=active), out_shape=(shape(3, active), shape(3, active)), name="final"
    )(parts)
    return (predicted, accel, jerk)


def interact(block, mine, gathered, message, active):
    stars, wide = mine.shape[1], message.shape[0] * active
    scalar = pl.BlockSpec(memory_space=pltpu.SMEM)
    vector = pl.BlockSpec(memory_space=pltpu.VMEM)
    own_result = pl.pallas_call(
        lambda *refs: own_kernel(*refs, active=active),
        out_shape=shape(8, wide),
        scratch_shapes=[pltpu.VMEM((7, stars, LANES), F32)],
        name="own",
    )(mine, message)
    steps = stars // STEP
    return pl.pallas_call(
        lambda *refs: main_kernel(*refs, active=active),
        out_shape=shape(message.shape[0], LANES),
        in_specs=[scalar, vector, vector, vector],
        scratch_shapes=[
            pltpu.VMEM((steps, 3, STEP, LANES), F32),
            pltpu.VMEM((wide // LANES, 48, LANES), F32),
            pltpu.VMEM((LANES, wide), BF16),
            pltpu.VMEM((32, wide), F32),
            pltpu.VMEM((32, wide), F32),
        ],
        name="interact",
    )(block, gathered, message, own_result)


def solution(mesh):
    whole = P(None, ("blk", "grp"))
    flat = P(("blk", "grp"))
    return jax.shard_map(
        local,
        mesh=mesh,
        in_specs=(whole, whole, whole, whole, flat, flat, flat),
        out_specs=(whole, whole, whole),
        check_vma=False,
    )
```

time: 102 us -> 81.2 us (0.80)
  Pallas kernels: 40.9 us -> 29.2 us
  local copies, waits for them, and re-layouts: 7.36 us -> 2.01 us
  waiting for transfers between devices: 8.15 us -> 4.32 us
  blocking collectives: 30.4 us -> 33.3 us
  other arithmetic: 1.41 us -> 0 us
  starting transfers between devices: 12.2 us -> 11.1 us
    pallas_call x2 -> x4, Pallas kernels: 40.9 us -> 29.2 us  [the longest x1 21.8 us: interact(): pl.pallas_call(lambda *refs: main_kernel(*refs, active=active), out_shape...]
    all_to_all x1, waiting for transfers between devices: 8.15 us -> 4.32 us  [local(): gathered = lax.all_to_all(sources, 'blk', 0, 0, tiled=True)]
    all_to_all x2, blocking collectives: 30.4 us -> 33.3 us  [the longest x1 18.7 us: local(): message = lax.all_to_all(targets, 'grp', 0, 0, tiled=True)]
    unnamed x11 -> x2, local copies, waits for them, and re-layouts: 3.16 us -> 0.69 us
    all_to_all x2 -> x0, other arithmetic: 1.37 us -> none  [the longest x1 0.68 us: local(): lax.all_to_all(result.reshape(members, active, 8), 'grp', 0, 0, tiled=True)]
    all_to_all x2 -> x0, local copies, waits for them, and re-layouts: 1.35 us -> none  [local(): targets = lax.all_to_all(targets, 'grp', 0, 0, tiled=True)]
    squeeze x0 -> x1, local copies, waits for them, and re-layouts: none -> 1.32 us  [local(): result = interact(block[None], sources[0], gathered, message, active)]
    all_to_all x1, starting transfers between devices: 12.2 us -> 11.1 us  [local(): gathered = lax.all_to_all(sources, 'blk', 0, 0, tiled=True)]
  transfers between devices with their start and end apart: 1 -> 1, of which waited for: 1 -> 1; matrix products, arithmetic and copies ran while one was open for 2% -> 2% of each run, Pallas kernels for 0% -> 5%
where the time goes in v2:
time: 81.2 us; the launch traced here: 80.5 us
  blocking collectives  33.3 us (41%)
  Pallas kernels  29.2 us (36%)
  starting transfers between devices  11.1 us (14%)
  waiting for transfers between devices  4.32 us (5%)
  local copies, waits for them, and re-layouts  2.01 us (2%)
    pallas_call x1, Pallas kernels, interact(): pl.pallas_call(lambda *refs: main_kernel(*refs, active=active), out_shape...  21.8 us
    all_to_all x1, blocking collectives, local(): message = lax.all_to_all(targets, 'grp', 0, 0, tiled=True)  18.7 us
    all_to_all x1, blocking collectives, local(): parts = lax.all_to_all(result, 'grp', 0, 0, tiled=True)  14.5 us
    all_to_all x1, starting transfers between devices, local(): gathered = lax.all_to_all(sources, 'blk', 0, 0, tiled=True)  11.1 us
    all_to_all x1, waiting for transfers between devices, local(): gathered = lax.all_to_all(sources, 'blk', 0, 0, tiled=True)  4.32 us
    pallas_call x1, Pallas kernels, interact(): pl.pallas_call(lambda *refs: own_kernel(*refs, active=active), out_shape=...  4.3 us
    pallas_call x1, Pallas kernels, local(): pl.pallas_call(prologue_kernel, out_shape=(shape(6, stars), shape(blocks,...  1.67 us
  transfers between devices with their start and end apart: 1, of which 1 were waited for; matrix products, arithmetic and copies ran while one was open for 2% of the time, Pallas kernels for 5%

profile of v2, /device:TPU:1, one launch (start us, length us, event | category | flops | bytes accessed | tf_op | source)
XLA Modules:
  0.0 80.5 jit_solution(6984924153791647483)
XLA Ops:
  0.6 1.7 %prologue.1 = (f32[6,512]{1,0:T(8,128)}, f32[16,8,512]{2,1,0:T(8,128)}, f32[32,128]{1,0:T(8,128)}) custom-call(s32[1]{0:T(128)} %bitcast.first, s32[1,16]{1,0:T(1,128)} %bitcast.22, f32[3,512]{1,0:T(4,128)} %position.1, f32[3,512]{1,0:T(4,128)} %velocity.1, f32[3,512]{1,0:T(4,128)} %accel_old.1, f32[3,512]{1,0:T(4,128)} %jerk_old.1, f32[1,512]{1,0:T(1,128)} %bitcast.20, ...), custom_call_target="tpu_custom_call" | custom-call | tf_op jit(solution)/shard_map/prologue/pallas_call | solution.py:269
  2.3 18.7 %all_to_all.27 = f32[32,1,128]{2,1,0:T(1,128)} all-to-all(f32[32,1,128]{2,1,0:T(1,128)} %bitcast.19), channel_id=1, replica_groups=mesh['blk'=16,'grp'=32] {'grp'}, dimensions={0} | all-to-all | bytes 32768 | tf_op jit(solution)/shard_map/all_to_all | solution.py:275
  21.0 11.1 %all-to-all-start = ((f32[16,8,512]{2,1,0:T(8,128)}), f32[16,8,512]{2,1,0:T(8,128)S(1)}, u32[]{:S(2)}, u32[]{:S(2)}) async-start(f32[16,8,512]{2,1,0:T(8,128)} %get-tuple-element.9), calls=%async_computation | async-start | bytes 524288 | tf_op jit(solution)/shard_map/all_to_all | solution.py:276
  32.1 1.3 %slice_bitcast_fusion.refs_0_ = f32[8,512]{1,0:T(8,128)} fusion(f32[16,8,512]{2,1,0:T(8,128)} %get-tuple-element.9), kind=kLoop, calls=%fused_computation | loop fusion | bytes 32768 | tf_op jit(solution)/shard_map/squeeze | solution.py:277
  33.5 4.3 %own.1.refs_3_ = f32[8,512]{1,0:T(8,128)} custom-call(f32[8,512]{1,0:T(8,128)} %slice_bitcast_fusion.refs_0_, f32[32,128]{1,0:T(8,128)} %bitcast.15), custom_call_target="tpu_custom_call" | custom-call | tf_op jit(solution)/shard_map/own/pallas_call | solution.py:289
  37.8 4.3 %all-to-all-done.refs_1_ = f32[16,8,512]{2,1,0:T(8,128)S(1)} async-done(((f32[16,8,512]{2,1,0:T(8,128)}), f32[16,8,512]{2,1,0:T(8,128)S(1)}, u32[]{:S(2)}, u32[]{:S(2)}) %all-to-all-start) | async-done | bytes 262176 | tf_op jit(solution)/shard_map/all_to_all | solution.py:276
  42.1 0.0 copy-start
  42.1 0.7 copy-done
  42.8 21.8 %interact.1 = f32[32,128]{1,0:T(8,128)} custom-call(s32[1]{0:T(128)} %bitcast.4.refs_0_, f32[16,8,512]{2,1,0:T(8,128)} %copy-done, f32[32,128]{1,0:T(8,128)} %bitcast.16, f32[8,512]{1,0:T(8,128)} %own.1.refs_3_), custom_call_target="tpu_custom_call" | custom-call | tf_op jit(solution)/shard_map/interact/pallas_call | solution.py:296
  64.6 14.5 %all_to_all.28 = f32[32,1,128]{2,1,0:T(1,128)} all-to-all(f32[32,1,128]{2,1,0:T(1,128)} %bitcast.17), channel_id=1, replica_groups=mesh['blk'=16,'grp'=32] {'grp'}, dimensions={0} | all-to-all | bytes 32768 | tf_op jit(solution)/shard_map/all_to_all | solution.py:278
  79.1 1.4 %final.1 = (f32[3,16]{1,0:T(4,128)}, f32[3,16]{1,0:T(4,128)}) custom-call(f32[32,128]{1,0:T(8,128)} %bitcast.18), custom_call_target="tpu_custom_call" | custom-call | tf_op jit(solution)/shard_map/final/pallas_call | solution.py:279
Async XLA Ops:
  21.0 21.0 %all-to-all-start = ((f32[16,8,512]{2,1,0:T(8,128)}), f32[16,8,512]{2,1,0:T(8,128)S(1)}, u32[]{:S(2)}, u32[]{:S(2)}) async-start(f32[16,8,512]{2,1,0:T(8,128)} %get-tuple-element.9), calls=%async_computation | async-start | bytes 524288 | tf_op jit(solution)/shard_map/all_to_all | solution.py:276
  42.1 0.7 copy-start

commit v3 on v2

--- a/solution.py
+++ b/solution.py
@@ -6,6 +6,7 @@
 from jax.sharding import PartitionSpec as P
 
 SOFTENING = 0.0001
+SQUARE_HALVES = ()
 LANES = 128
 STEP = 256
 F32 = jnp.float32
@@ -37,7 +38,7 @@
     new_velocity = velocity[...] + step_row * accel_old[...] + half * jerk_old[...]
     predicted[0:3, :] = new_position
     predicted[3:6, :] = new_velocity
-    everything = jnp.concatenate([new_position, new_velocity, mass[...], jnp.ones_like(step_row)], 0)
+    everything = jnp.concatenate([new_position, jnp.ones_like(step_row), new_velocity, mass[...]], 0)
     for copy in range(sources.shape[0]):
         sources[copy] = everything
     offsets = active_index[...] - first[0]
@@ -45,6 +46,7 @@
     high, middle, low = in_three(everything)
     dot = lambda piece: jnp.dot(piece, chosen, preferred_element_type=F32)
     picked = (dot(high) + dot(middle)) + dot(low)
+    picked = jnp.concatenate([picked[0:3], picked[4:7], picked[0:2]], 0)
     picked = jnp.concatenate([picked, jnp.zeros((8, LANES - active), F32)], 1)
     spread = pltpu.roll(picked, 0, 1, stride=active, stride_axis=0)
     line = jnp.sum(spread, 0, keepdims=True)
@@ -78,66 +80,111 @@
         result[group * 8 : group * 8 + 8, :] = total
 
 
-def radial_features(state, first_order):
-    row = row_iota(state.shape)
-    grid = jnp.where(row < 3, 1.5 * 2.0**20, 1.5 * 2.0**14)
+def exact(value):
+    return value.astype(BF16).astype(F32)
+
+
+def three_parts(value):
+    high = exact(value)
+    rest = value - high
+    middle = exact(rest)
+    return high, middle, rest - middle
+
+
+def halves(upper, lower):
+    return jnp.where(row_iota(upper.shape) < 4, upper, lower)
+
+
+def swap(value):
+    return pltpu.roll(value, 4, 0)
+
+
+def with_one(value):
+    return jnp.where(row_iota(value.shape) == 3, 1.0, value)
+
+
+def constant_groups(product, mixed):
+    p, m = three_parts(product), three_parts(mixed)
+    return with_one(halves(p[0], p[1])), with_one(halves(p[2], m[0])), halves(m[1], m[2])
+
+
+def radial_parts(state):
+    grid = jnp.where(row_iota(state.shape) < 4, 1.5 * 2.0**20, 1.5 * 2.0**14)
     coarse = (state + grid) - grid
     fine = state - coarse
-    exact = lambda value: value.astype(BF16).astype(F32)
     top = exact(coarse)
     bottom = coarse - top
+    first, second, third = three_parts(fine)
+    product = coarse * swap(coarse)
+    cross = coarse * swap(fine)
+    mixed = (cross + swap(cross)) + fine * swap(fine)
+    before = [top, halves(top, bottom)]
+    after = [halves(top, first), halves(top, second), halves(first, top), halves(first, bottom), first]
+    after += [halves(second, top), halves(second, bottom), halves(third, top)]
+    return before, after, product, mixed
+
+
+def square_parts(state):
+    both = halves(state, swap(state))
+    coarse = (both + 1.5 * 2.0**17) - 1.5 * 2.0**17
+    fine = both - coarse
+    upper = (coarse + 1.5 * 2.0**21) - 1.5 * 2.0**21
+    lower = coarse - upper
     first = exact(fine)
-    second = exact(fine - first)
-    third = fine - first - second
-    line = lambda value, k: value[k : k + 1]
-    both = [line(coarse, k) * line(coarse, k + 3) for k in range(3)]
-    whole = both[0] + both[1] + both[2]
-    mixed = [line(coarse, k) * line(fine, k + 3) + line(fine, k) * line(state, k + 3) for k in range(3)]
-    part = mixed[0] + mixed[1] + mixed[2]
-    pieces = []
-    for value in (whole, part):
-        high = exact(value)
-        middle = exact(value - high)
-        pieces.append((high, middle, value - high - middle))
-    pick = lambda upper, lower: jnp.where(row < 3, upper, lower)
-    zero = jnp.zeros_like(state)
-    groups = [
-        (top, pieces[0][0]),
-        (pick(top, bottom), pieces[0][1]),
-        (zero, pieces[0][2]),
-        (pick(top, first), pieces[1][0]),
-        (pick(top, second), pieces[1][1]),
-        (pick(first, top), pieces[1][2]),
-        (pick(first, bottom), None),
-        (first, None),
-        (pick(second, top), None),
-        (pick(second, bottom), None),
-        (pick(third, top), None),
-    ]
-    rows = []
-    for value, extra in groups:
-        if not first_order:
-            value = -jnp.concatenate([value[3:6], value[0:3], value[6:8]], 0)
-        if extra is None:
-            value = jnp.where(row < 6, value, 0.0)
-        else:
-            wide = jnp.broadcast_to(extra, value.shape)
-            value = jnp.where(row < 6, value, jnp.where(row == (6 if first_order else 7), wide, 1.0))
-        rows.append(value)
-    rows += [zero] * (16 - len(rows))
-    return jnp.concatenate(rows, 0)
-
-
-def spread_columns(block, spread, count):
+    return upper, lower, first, fine - first, coarse * coarse, fine * ((coarse + coarse) + fine)
+
+
+def stack(groups):
+    return jnp.concatenate(groups + [jnp.zeros_like(groups[0])] * (16 - len(groups)), 0)
+
+
+def source_features(state):
+    before, after, product, mixed = radial_parts(state)
+    one, two, last = constant_groups(product, mixed)
+    radial = stack(before + [one, two] + after + [last])
+    upper, lower, first, second, product, mixed = square_parts(state)
+    one, two, last = constant_groups(product, mixed)
+    a, b = halves(upper, lower), halves(first, second)
+    return radial, stack([a, a, one, two, a, a, b, b, b, b, last])
+
+
+def target_features(state):
+    row = row_iota(state.shape)
+    inside = (row != 3) & (row != 7)
+    ones = jnp.where(inside, 1.0, 0.0)
+
+    def constants(product, mixed, extra):
+        add = lambda value: value[0:1] + value[1:2] + value[2:3]
+        return three_parts(add(product)) + three_parts(add(mixed) + extra)
+
+    def filled(group, value):
+        group = jnp.where(inside, group, 0.0)
+        return group if value is None else jnp.where(row == 3, jnp.broadcast_to(value, group.shape), group)
+
+    before, after, product, mixed = radial_parts(state)
+    c = constants(product, mixed, 0.0)
+    flip = lambda group: -swap(group)
+    radial = [filled(flip(before[0]), c[0]), filled(flip(before[1]), c[1]), filled(ones, c[2]), filled(ones, c[3])]
+    radial += [filled(flip(after[0]), c[4]), filled(flip(after[1]), c[5])] + [filled(flip(group), None) for group in after[2:]]
+    upper, lower, first, second, product, mixed = square_parts(state)
+    c = constants(product, mixed, SOFTENING)
+    pair = lambda a, b: -2.0 * halves(a, b)
+    square = [filled(pair(upper, lower), c[0]), filled(pair(lower, upper), c[1]), filled(ones, c[2]), filled(ones, c[3])]
+    square += [filled(pair(first, first), c[4]), filled(pair(second, second), c[5])]
+    square += [filled(pair(a, b), None) for a, b in ((upper, upper), (lower, lower), (first, first), (second, 0.0 * second))]
+    return stack(radial + [ones]), stack(square + [ones])
+
+
+def spread_columns(block, spread, picks):
     columns = block.T
     for row in range(0, columns.shape[0], 8):
-        for k in range(count):
-            spread[k, row : row + 8, :] = jnp.broadcast_to(columns[row : row + 8, k : k + 1], (8, LANES))
+        for k, pick in enumerate(picks):
+            spread[k, row : row + 8, :] = jnp.broadcast_to(columns[row : row + 8, pick : pick + 1], (8, LANES))
 
 
 def own_kernel(sources, message, result, spread, *, active):
     stars = sources.shape[1]
-    spread_columns(sources[...], spread, 7)
+    spread_columns(sources[...], spread, (0, 1, 2, 4, 5, 6, 7))
     lines = unpack_targets(message[...], active)
     wide = message.shape[0] * active
     total = []
@@ -171,16 +218,20 @@
     result[...] = jnp.concatenate(rows + rows[:2], 0)
 
 
-def main_kernel(block, sources, message, own_result, result, spread, target_rows, target_side, sum_w, sum_d, *, active):
+def main_kernel(block, sources, message, own_result, result, spread, target_rows, radial_side, square_side, sum_w, sum_d, *, active):
     blocks, stars = sources.shape[0], sources.shape[2]
     wide = message.shape[0] * active
     groups = wide // LANES
     lines = unpack_targets(message[...], active)
-    target_side[...] = radial_features(jnp.concatenate(lines + lines[:2], 0), False).astype(BF16)
+    blank = jnp.zeros_like(lines[0])
+    radial, square = target_features(jnp.concatenate(lines[:3] + [blank + 1.0] + lines[3:] + [blank], 0))
+    radial_side[...] = radial.astype(BF16)
+    square_side[...] = square.astype(BF16)
     middle_of = lambda line: 0.5 * (jnp.min(line, 1, keepdims=True) + jnp.max(line, 1, keepdims=True))
     centers = [middle_of(line) for line in lines]
-    center = jnp.concatenate(centers + [jnp.zeros((2, 1), F32)], 0)
-    for k, row in enumerate(lines):
+    nothing = jnp.zeros((1, 1), F32)
+    center = jnp.concatenate(centers[:3] + [nothing] + centers[3:] + [nothing], 0)
+    for k, row in enumerate(lines[:3]):
         for g in range(groups):
             target_rows[g, k * 8 : k * 8 + 8, :] = jnp.broadcast_to(row[:, g * LANES : g * LANES + LANES], (8, LANES))
     sum_w[...] = jnp.zeros(sum_w.shape, F32)
@@ -189,31 +240,38 @@
     def one_block(turn, unused):
         chunk = lax.rem(block[0] + 1 + turn, blocks)
         here = sources[chunk]
-        scaled = (here - center) * here[6:7]
+        scaled = (here - center) * here[7:8]
         high, middle, low = in_three(scaled)
         stacked = jnp.concatenate([high.astype(F32), middle.astype(F32), low.astype(F32), jnp.zeros_like(scaled)], 0).astype(BF16)
-        source_side = radial_features(here, True).T.astype(BF16)
+        radial, square = source_features(here)
+        radial = radial.T.astype(BF16)
+        square = square.T.astype(BF16)
         for step in range(stars // STEP):
-            spread_columns(here[:, step * STEP : step * STEP + STEP], spread.at[step], 3)
+            spread_columns(here[:, step * STEP : step * STEP + STEP], spread.at[step], (0, 1, 2))
             part = stacked[:, step * STEP : step * STEP + STEP]
             left = jnp.concatenate([part, part], 1)
             for half in range(groups // 2):
                 lanes = slice(half * 2 * LANES, half * 2 * LANES + 2 * LANES)
-                products = jnp.dot(
-                    source_side[step * STEP : step * STEP + STEP], target_side[:, lanes], preferred_element_type=F32
-                )
+                some = slice(step * STEP, step * STEP + STEP)
+                products = jnp.dot(radial[some], radial_side[:, lanes], preferred_element_type=F32)
+                by_product = half in SQUARE_HALVES
+                if by_product:
+                    squares = jnp.dot(square[some], square_side[:, lanes], preferred_element_type=F32)
                 full = [[], [], [], []]
                 for row in range(0, STEP, 16):
                     across = [[], [], [], []]
                     for g in (2 * half, 2 * half + 1):
-                        own = [target_rows[g, k * 8 : k * 8 + 8, :] for k in range(3)]
+                        own = None if by_product else [target_rows[g, k * 8 : k * 8 + 8, :] for k in range(3)]
                         at_lane = (g - 2 * half) * LANES
                         both_w, both_d = [], []
                         for sub in range(2):
                             top = row + sub * 8
-                            there = [spread[step, k, top : top + 8, :] for k in range(3)]
-                            r = [there[k] - own[k] for k in range(3)]
-                            q = r[0] * r[0] + r[1] * r[1] + (r[2] * r[2] + SOFTENING)
+                            if by_product:
+                                q = squares[top : top + 8, at_lane : at_lane + LANES]
+                            else:
+                                there = [spread[step, k, top : top + 8, :] for k in range(3)]
+                                r = [there[k] - own[k] for k in range(3)]
+                                q = r[0] * r[0] + r[1] * r[1] + (r[2] * r[2] + SOFTENING)
                             s = products[top : top + 8, at_lane : at_lane + LANES]
                             inverse = lax.rsqrt(q)
                             squared = inverse * inverse
@@ -233,17 +291,16 @@
                 sum_d[:, lanes] += jnp.dot(left, right_d, preferred_element_type=F32)
         return unused
 
-    lax.fori_loop(0, blocks - 1, one_block, 0)
+    lax.fori_loop(0, blocks - 1, one_block, 0, unroll=5)
     total_w = sum_w[0:8] + (sum_w[8:16] + sum_w[16:24])
     total_d = sum_d[0:8] + (sum_d[8:16] + sum_d[16:24])
-    here = [jnp.concatenate([target_rows[g, k * 8 : k * 8 + 1, :] for g in range(groups)], 1) for k in range(6)]
-    here = [value - middle for value, middle in zip(here, centers)]
+    here = [value - middle for value, middle in zip(lines, centers)]
     rows = []
     for k in range(3):
-        rows.append(own_result[k : k + 1] + (total_w[k : k + 1] - here[k] * total_w[7:8]))
+        rows.append(own_result[k : k + 1] + (total_w[k : k + 1] - here[k] * total_w[3:4]))
     for k in range(3):
-        straight = total_w[k + 3 : k + 4] - here[k + 3] * total_w[7:8]
-        inward = total_d[k : k + 1] - here[k] * total_d[7:8]
+        straight = total_w[k + 4 : k + 5] - here[k + 3] * total_w[3:4]
+        inward = total_d[k : k + 1] - here[k] * total_d[3:4]
         rows.append(own_result[k + 3 : k + 4] + (straight - 3.0 * inward))
     pack_results(rows, active, result)
 
@@ -299,7 +356,8 @@
         in_specs=[scalar, vector, vector, vector],
         scratch_shapes=[
             pltpu.VMEM((steps, 3, STEP, LANES), F32),
-            pltpu.VMEM((wide // LANES, 48, LANES), F32),
+            pltpu.VMEM((wide // LANES, 24, LANES), F32),
+            pltpu.VMEM((LANES, wide), BF16),
             pltpu.VMEM((LANES, wide), BF16),
             pltpu.VMEM((32, wide), F32),
             pltpu.VMEM((32, wide), F32),

time: 81.2 us -> 76.4 us (0.941)
  Pallas kernels: 29.2 us -> 24.3 us
    pallas_call x1, Pallas kernels: 21.8 us -> 16.9 us  [interact(): pl.pallas_call(lambda *refs: main_kernel(*refs, active=active), out_shape...]
  transfers between devices with their start and end apart: 1 -> 1, of which waited for: 1 -> 1; matrix products, arithmetic and copies ran while one was open for 2% -> 2% of each run, Pallas kernels for 5% -> 6%
where the time goes in v3:
time: 76.4 us; the launch traced here: 75.6 us
  blocking collectives  33.2 us (43%)
  Pallas kernels  24.3 us (32%)
  starting transfers between devices  11.1 us (15%)
  waiting for transfers between devices  4.32 us (6%)
  local copies, waits for them, and re-layouts  2.01 us (3%)
    all_to_all x1, blocking collectives, local(): message = lax.all_to_all(targets, 'grp', 0, 0, tiled=True)  18.7 us
    pallas_call x1, Pallas kernels, interact(): pl.pallas_call(lambda *refs: main_kernel(*refs, active=active), out_shape...  16.9 us
    all_to_all x1, blocking collectives, local(): parts = lax.all_to_all(result, 'grp', 0, 0, tiled=True)  14.5 us
    all_to_all x1, starting transfers between devices, local(): gathered = lax.all_to_all(sources, 'blk', 0, 0, tiled=True)  11.1 us
    all_to_all x1, waiting for transfers between devices, local(): gathered = lax.all_to_all(sources, 'blk', 0, 0, tiled=True)  4.32 us
    pallas_call x1, Pallas kernels, interact(): pl.pallas_call(lambda *refs: own_kernel(*refs, active=active), out_shape=...  4.3 us
    pallas_call x1, Pallas kernels, local(): pl.pallas_call(prologue_kernel, out_shape=(shape(6, stars), shape(blocks,...  1.67 us
  transfers between devices with their start and end apart: 1, of which 1 were waited for; matrix products, arithmetic and copies ran while one was open for 2% of the time, Pallas kernels for 6%

profile of v3, /device:TPU:1, one launch (start us, length us, event | category | flops | bytes accessed | tf_op | source)
XLA Modules:
  0.0 75.6 jit_solution(9053704751176134582)
XLA Ops:
  0.6 1.7 %prologue.1 = (f32[6,512]{1,0:T(8,128)}, f32[16,8,512]{2,1,0:T(8,128)}, f32[32,128]{1,0:T(8,128)}) custom-call(s32[1]{0:T(128)} %bitcast.first, s32[1,16]{1,0:T(1,128)} %bitcast.22, f32[3,512]{1,0:T(4,128)} %position.1, f32[3,512]{1,0:T(4,128)} %velocity.1, f32[3,512]{1,0:T(4,128)} %accel_old.1, f32[3,512]{1,0:T(4,128)} %jerk_old.1, f32[1,512]{1,0:T(1,128)} %bitcast.20, ...), custom_call_target="tpu_custom_call" | custom-call | tf_op jit(solution)/shard_map/prologue/pallas_call | solution.py:326
  2.3 18.7 %all_to_all.27 = f32[32,1,128]{2,1,0:T(1,128)} all-to-all(f32[32,1,128]{2,1,0:T(1,128)} %bitcast.19), channel_id=1, replica_groups=mesh['blk'=16,'grp'=32] {'grp'}, dimensions={0} | all-to-all | bytes 32768 | tf_op jit(solution)/shard_map/all_to_all | solution.py:332
  21.0 11.1 %all-to-all-start = ((f32[16,8,512]{2,1,0:T(8,128)}), f32[16,8,512]{2,1,0:T(8,128)S(1)}, u32[]{:S(2)}, u32[]{:S(2)}) async-start(f32[16,8,512]{2,1,0:T(8,128)} %get-tuple-element.9), calls=%async_computation | async-start | bytes 524288 | tf_op jit(solution)/shard_map/all_to_all | solution.py:333
  32.1 1.3 %slice_bitcast_fusion.refs_0_ = f32[8,512]{1,0:T(8,128)} fusion(f32[16,8,512]{2,1,0:T(8,128)} %get-tuple-element.9), kind=kLoop, calls=%fused_computation | loop fusion | bytes 32768 | tf_op jit(solution)/shard_map/squeeze | solution.py:334
  33.5 4.3 %own.1.refs_3_ = f32[8,512]{1,0:T(8,128)} custom-call(f32[8,512]{1,0:T(8,128)} %slice_bitcast_fusion.refs_0_, f32[32,128]{1,0:T(8,128)} %bitcast.15), custom_call_target="tpu_custom_call" | custom-call | tf_op jit(solution)/shard_map/own/pallas_call | solution.py:346
  37.8 4.3 %all-to-all-done.refs_1_ = f32[16,8,512]{2,1,0:T(8,128)S(1)} async-done(((f32[16,8,512]{2,1,0:T(8,128)}), f32[16,8,512]{2,1,0:T(8,128)S(1)}, u32[]{:S(2)}, u32[]{:S(2)}) %all-to-all-start) | async-done | bytes 262176 | tf_op jit(solution)/shard_map/all_to_all | solution.py:333
  42.1 0.0 copy-start
  42.1 0.7 copy-done
  42.8 16.9 %interact.1 = f32[32,128]{1,0:T(8,128)} custom-call(s32[1]{0:T(128)} %bitcast.4.refs_0_, f32[16,8,512]{2,1,0:T(8,128)} %copy-done, f32[32,128]{1,0:T(8,128)} %bitcast.16, f32[8,512]{1,0:T(8,128)} %own.1.refs_3_), custom_call_target="tpu_custom_call" | custom-call | tf_op jit(solution)/shard_map/interact/pallas_call | solution.py:353
  59.7 14.5 %all_to_all.28 = f32[32,1,128]{2,1,0:T(1,128)} all-to-all(f32[32,1,128]{2,1,0:T(1,128)} %bitcast.17), channel_id=1, replica_groups=mesh['blk'=16,'grp'=32] {'grp'}, dimensions={0} | all-to-all | bytes 32768 | tf_op jit(solution)/shard_map/all_to_all | solution.py:335
  74.2 1.4 %final.1 = (f32[3,16]{1,0:T(4,128)}, f32[3,16]{1,0:T(4,128)}) custom-call(f32[32,128]{1,0:T(8,128)} %bitcast.18), custom_call_target="tpu_custom_call" | custom-call | tf_op jit(solution)/shard_map/final/pallas_call | solution.py:336
Async XLA Ops:
  21.0 21.0 %all-to-all-start = ((f32[16,8,512]{2,1,0:T(8,128)}), f32[16,8,512]{2,1,0:T(8,128)S(1)}, u32[]{:S(2)}, u32[]{:S(2)}) async-start(f32[16,8,512]{2,1,0:T(8,128)} %get-tuple-element.9), calls=%async_computation | async-start | bytes 524288 | tf_op jit(solution)/shard_map/all_to_all | solution.py:333
  42.1 0.7 copy-start

commit v4 on v3

--- a/solution.py
+++ b/solution.py
@@ -6,7 +6,6 @@
 from jax.sharding import PartitionSpec as P
 
 SOFTENING = 0.0001
-SQUARE_HALVES = ()
 LANES = 128
 STEP = 256
 F32 = jnp.float32
@@ -29,7 +28,7 @@
     return lax.broadcasted_iota(jnp.int32, shape, 0)
 
 
-def prologue_kernel(first, active_index, position, velocity, accel_old, jerk_old, mass, elapsed, predicted, sources, targets):
+def prologue_kernel(first, active_index, position, velocity, accel_old, jerk_old, mass, elapsed, predicted, sources, targets, mine):
     active, stars = active_index.shape[1], position.shape[1]
     step_row = elapsed[...]
     half = step_row * step_row * 0.5
@@ -39,6 +38,7 @@
     predicted[0:3, :] = new_position
     predicted[3:6, :] = new_velocity
     everything = jnp.concatenate([new_position, jnp.ones_like(step_row), new_velocity, mass[...]], 0)
+    mine[...] = everything
     for copy in range(sources.shape[0]):
         sources[copy] = everything
     offsets = active_index[...] - first[0]
@@ -124,16 +124,6 @@
     return before, after, product, mixed
 
 
-def square_parts(state):
-    both = halves(state, swap(state))
-    coarse = (both + 1.5 * 2.0**17) - 1.5 * 2.0**17
-    fine = both - coarse
-    upper = (coarse + 1.5 * 2.0**21) - 1.5 * 2.0**21
-    lower = coarse - upper
-    first = exact(fine)
-    return upper, lower, first, fine - first, coarse * coarse, fine * ((coarse + coarse) + fine)
-
-
 def stack(groups):
     return jnp.concatenate(groups + [jnp.zeros_like(groups[0])] * (16 - len(groups)), 0)
 
@@ -141,11 +131,7 @@
 def source_features(state):
     before, after, product, mixed = radial_parts(state)
     one, two, last = constant_groups(product, mixed)
-    radial = stack(before + [one, two] + after + [last])
-    upper, lower, first, second, product, mixed = square_parts(state)
-    one, two, last = constant_groups(product, mixed)
-    a, b = halves(upper, lower), halves(first, second)
-    return radial, stack([a, a, one, two, a, a, b, b, b, b, last])
+    return stack(before + [one, two] + after + [last])
 
 
 def target_features(state):
@@ -153,26 +139,20 @@
     inside = (row != 3) & (row != 7)
     ones = jnp.where(inside, 1.0, 0.0)
 
-    def constants(product, mixed, extra):
+    def constants(product, mixed):
         add = lambda value: value[0:1] + value[1:2] + value[2:3]
-        return three_parts(add(product)) + three_parts(add(mixed) + extra)
+        return three_parts(add(product)) + three_parts(add(mixed))
 
     def filled(group, value):
         group = jnp.where(inside, group, 0.0)
         return group if value is None else jnp.where(row == 3, jnp.broadcast_to(value, group.shape), group)
 
     before, after, product, mixed = radial_parts(state)
-    c = constants(product, mixed, 0.0)
+    c = constants(product, mixed)
     flip = lambda group: -swap(group)
     radial = [filled(flip(before[0]), c[0]), filled(flip(before[1]), c[1]), filled(ones, c[2]), filled(ones, c[3])]
     radial += [filled(flip(after[0]), c[4]), filled(flip(after[1]), c[5])] + [filled(flip(group), None) for group in after[2:]]
-    upper, lower, first, second, product, mixed = square_parts(state)
-    c = constants(product, mixed, SOFTENING)
-    pair = lambda a, b: -2.0 * halves(a, b)
-    square = [filled(pair(upper, lower), c[0]), filled(pair(lower, upper), c[1]), filled(ones, c[2]), filled(ones, c[3])]
-    square += [filled(pair(first, first), c[4]), filled(pair(second, second), c[5])]
-    square += [filled(pair(a, b), None) for a, b in ((upper, upper), (lower, lower), (first, first), (second, 0.0 * second))]
-    return stack(radial + [ones]), stack(square + [ones])
+    return stack(radial + [ones])
 
 
 def spread_columns(block, spread, picks):
@@ -182,11 +162,22 @@
             spread[k, row : row + 8, :] = jnp.broadcast_to(columns[row : row + 8, pick : pick + 1], (8, LANES))
 
 
-def own_kernel(sources, message, result, spread, *, active):
+def own_kernel(sources, message, result, here, center, target_rows, radial_side, spread, *, active):
     stars = sources.shape[1]
     spread_columns(sources[...], spread, (0, 1, 2, 4, 5, 6, 7))
     lines = unpack_targets(message[...], active)
     wide = message.shape[0] * active
+    blank = jnp.zeros_like(lines[0])
+    state = jnp.concatenate(lines[:3] + [blank + 1.0] + lines[3:] + [blank], 0)
+    radial_side[...] = target_features(state).astype(BF16)
+    middle = 0.5 * (jnp.min(state, 1, keepdims=True) + jnp.max(state, 1, keepdims=True))
+    row = row_iota(state.shape)
+    middle = jnp.where((row == 3) | (row == 7), 0.0, jnp.broadcast_to(middle, state.shape))
+    here[...] = state - middle
+    center[...] = middle[:, :LANES]
+    for k, line in enumerate(lines[:3]):
+        for g in range(wide // LANES):
+            target_rows[g, k * 8 : k * 8 + 8, :] = jnp.broadcast_to(line[:, g * LANES : g * LANES + LANES], (8, LANES))
     total = []
     for group in range(wide // LANES):
         own = [jnp.broadcast_to(line[:, group * LANES : group * LANES + LANES], (8, LANES)) for line in lines]
@@ -218,34 +209,19 @@
     result[...] = jnp.concatenate(rows + rows[:2], 0)
 
 
-def main_kernel(block, sources, message, own_result, result, spread, target_rows, radial_side, square_side, sum_w, sum_d, *, active):
+def main_kernel(block, sources, own_result, here_rows, center, target_rows, radial_side, result, spread, sum_w, sum_d, *, active):
     blocks, stars = sources.shape[0], sources.shape[2]
-    wide = message.shape[0] * active
-    groups = wide // LANES
-    lines = unpack_targets(message[...], active)
-    blank = jnp.zeros_like(lines[0])
-    radial, square = target_features(jnp.concatenate(lines[:3] + [blank + 1.0] + lines[3:] + [blank], 0))
-    radial_side[...] = radial.astype(BF16)
-    square_side[...] = square.astype(BF16)
-    middle_of = lambda line: 0.5 * (jnp.min(line, 1, keepdims=True) + jnp.max(line, 1, keepdims=True))
-    centers = [middle_of(line) for line in lines]
-    nothing = jnp.zeros((1, 1), F32)
-    center = jnp.concatenate(centers[:3] + [nothing] + centers[3:] + [nothing], 0)
-    for k, row in enumerate(lines[:3]):
-        for g in range(groups):
-            target_rows[g, k * 8 : k * 8 + 8, :] = jnp.broadcast_to(row[:, g * LANES : g * LANES + LANES], (8, LANES))
+    groups = here_rows.shape[1] // LANES
     sum_w[...] = jnp.zeros(sum_w.shape, F32)
     sum_d[...] = jnp.zeros(sum_d.shape, F32)
 
     def one_block(turn, unused):
         chunk = lax.rem(block[0] + 1 + turn, blocks)
         here = sources[chunk]
-        scaled = (here - center) * here[7:8]
+        scaled = (here - center[:, :1]) * here[7:8]
         high, middle, low = in_three(scaled)
         stacked = jnp.concatenate([high.astype(F32), middle.astype(F32), low.astype(F32), jnp.zeros_like(scaled)], 0).astype(BF16)
-        radial, square = source_features(here)
-        radial = radial.T.astype(BF16)
-        square = square.T.astype(BF16)
+        radial = source_features(here).T.astype(BF16)
         for step in range(stars // STEP):
             spread_columns(here[:, step * STEP : step * STEP + STEP], spread.at[step], (0, 1, 2))
             part = stacked[:, step * STEP : step * STEP + STEP]
@@ -254,24 +230,18 @@
                 lanes = slice(half * 2 * LANES, half * 2 * LANES + 2 * LANES)
                 some = slice(step * STEP, step * STEP + STEP)
                 products = jnp.dot(radial[some], radial_side[:, lanes], preferred_element_type=F32)
-                by_product = half in SQUARE_HALVES
-                if by_product:
-                    squares = jnp.dot(square[some], square_side[:, lanes], preferred_element_type=F32)
                 full = [[], [], [], []]
                 for row in range(0, STEP, 16):
                     across = [[], [], [], []]
                     for g in (2 * half, 2 * half + 1):
-                        own = None if by_product else [target_rows[g, k * 8 : k * 8 + 8, :] for k in range(3)]
+                        own = [target_rows[g, k * 8 : k * 8 + 8, :] for k in range(3)]
                         at_lane = (g - 2 * half) * LANES
                         both_w, both_d = [], []
                         for sub in range(2):
                             top = row + sub * 8
-                            if by_product:
-                                q = squares[top : top + 8, at_lane : at_lane + LANES]
-                            else:
-                                there = [spread[step, k, top : top + 8, :] for k in range(3)]
-                                r = [there[k] - own[k] for k in range(3)]
-                                q = r[0] * r[0] + r[1] * r[1] + (r[2] * r[2] + SOFTENING)
+                            there = [spread[step, k, top : top + 8, :] for k in range(3)]
+                            r = [there[k] - own[k] for k in range(3)]
+                            q = r[0] * r[0] + r[1] * r[1] + (r[2] * r[2] + SOFTENING)
                             s = products[top : top + 8, at_lane : at_lane + LANES]
                             inverse = lax.rsqrt(q)
                             squared = inverse * inverse
@@ -294,7 +264,7 @@
     lax.fori_loop(0, blocks - 1, one_block, 0, unroll=5)
     total_w = sum_w[0:8] + (sum_w[8:16] + sum_w[16:24])
     total_d = sum_d[0:8] + (sum_d[8:16] + sum_d[16:24])
-    here = [value - middle for value, middle in zip(lines, centers)]
+    here = [here_rows[k : k + 1] for k in (0, 1, 2, 4, 5, 6)]
     rows = []
     for k in range(3):
         rows.append(own_result[k : k + 1] + (total_w[k : k + 1] - here[k] * total_w[3:4]))
@@ -312,6 +282,14 @@
         (accel if k < 3 else jerk)[k % 3 : k % 3 + 1, :] = turned[k : k + 1, :active]
 
 
+def keep_near(value):
+    return pltpu.with_memory_space_constraint(value, pltpu.VMEM)
+
+
+def near(*lengths):
+    return pltpu.VMEM(lengths, F32)
+
+
 def shape(*lengths):
     return jax.ShapeDtypeStruct(lengths, F32)
 
@@ -323,16 +301,17 @@
     first = ((block * members + lax.axis_index("grp")) * stars)[None]
     scalar = pl.BlockSpec(memory_space=pltpu.SMEM)
     vector = pl.BlockSpec(memory_space=pltpu.VMEM)
-    predicted, sources, targets = pl.pallas_call(
+    predicted, sources, targets, mine = pl.pallas_call(
         prologue_kernel,
-        out_shape=(shape(6, stars), shape(blocks, 8, stars), shape(members, LANES)),
+        out_shape=(shape(6, stars), shape(blocks, 8, stars), near(members, LANES), near(8, stars)),
         in_specs=[scalar] + [vector] * 7,
         name="prologue",
     )(first, active_index[None], position, velocity, accel_old, jerk_old, mass[None], elapsed[None])
     message = lax.all_to_all(targets, "grp", 0, 0, tiled=True)
     gathered = lax.all_to_all(sources, "blk", 0, 0, tiled=True)
-    result = interact(block[None], sources[0], gathered, message, active)
+    result = interact(block[None], mine, gathered, message, active)
     parts = lax.all_to_all(result, "grp", 0, 0, tiled=True)
+    parts = keep_near(parts)
     accel, jerk = pl.pallas_call(
         lambda *refs: final_kernel(*refs, active=active), out_shape=(shape(3, active), shape(3, active)), name="final"
     )(parts)
@@ -341,29 +320,27 @@
 
 def interact(block, mine, gathered, message, active):
     stars, wide = mine.shape[1], message.shape[0] * active
+    groups = wide // LANES
     scalar = pl.BlockSpec(memory_space=pltpu.SMEM)
     vector = pl.BlockSpec(memory_space=pltpu.VMEM)
-    own_result = pl.pallas_call(
+    mine, message = keep_near(mine), keep_near(message)
+    prepared = pl.pallas_call(
         lambda *refs: own_kernel(*refs, active=active),
-        out_shape=shape(8, wide),
+        out_shape=(near(8, wide), near(8, wide), near(8, LANES), near(groups, 24, LANES), pltpu.VMEM((LANES, wide), BF16)),
         scratch_shapes=[pltpu.VMEM((7, stars, LANES), F32)],
         name="own",
     )(mine, message)
-    steps = stars // STEP
     return pl.pallas_call(
         lambda *refs: main_kernel(*refs, active=active),
-        out_shape=shape(message.shape[0], LANES),
-        in_specs=[scalar, vector, vector, vector],
+        out_shape=near(message.shape[0], LANES),
+        in_specs=[scalar] + [vector] * 6,
         scratch_shapes=[
-            pltpu.VMEM((steps, 3, STEP, LANES), F32),
-            pltpu.VMEM((wide // LANES, 24, LANES), F32),
-            pltpu.VMEM((LANES, wide), BF16),
-            pltpu.VMEM((LANES, wide), BF16),
+            pltpu.VMEM((stars // STEP, 3, STEP, LANES), F32),
             pltpu.VMEM((32, wide), F32),
             pltpu.VMEM((32, wide), F32),
         ],
         name="interact",
-    )(block, gathered, message, own_result)
+    )(block, keep_near(gathered), *[keep_near(value) for value in prepared])
 
 
 def solution(mesh):

time: 76.4 us -> 71.1 us (0.931)
  Pallas kernels: 24.3 us -> 20.2 us
  waiting for transfers between devices: 4.32 us -> 7.31 us
  blocking collectives: 33.2 us -> 30.4 us
  local copies, waits for them, and re-layouts: 2.01 us -> 0 us
  starting transfers between devices: 11.1 us -> 12.2 us
    all_to_all x1, waiting for transfers between devices: 4.32 us -> 7.31 us  [local(): gathered = lax.all_to_all(sources, 'blk', 0, 0, tiled=True)]
    pallas_call x1, Pallas kernels: 16.9 us -> 15 us  [interact(): pl.pallas_call(lambda *refs: main_kernel(*refs, active=active), out_shape...]
    all_to_all x1, blocking collectives: 14.5 us -> 12.9 us  [local(): parts = lax.all_to_all(result, 'grp', 0, 0, tiled=True)]
    pallas_call x1, Pallas kernels: 4.3 us -> 2.97 us  [interact(): pl.pallas_call(lambda *refs: own_kernel(*refs, active=active), out_shape=...]
    squeeze x1 -> x0, local copies, waits for them, and re-layouts: 1.32 us -> none  [local(): result = interact(block[None], sources[0], gathered, message, active)]
    all_to_all x1, blocking collectives: 18.7 us -> 17.5 us  [local(): message = lax.all_to_all(targets, 'grp', 0, 0, tiled=True)]
    all_to_all x1, starting transfers between devices: 11.1 us -> 12.2 us  [local(): gathered = lax.all_to_all(sources, 'blk', 0, 0, tiled=True)]
  transfers between devices with their start and end apart: 1 -> 1, of which waited for: 1 -> 1; matrix products, arithmetic and copies ran while one was open for 2% -> 0% of each run, Pallas kernels for 6% -> 4%
where the time goes in v4:
time: 71.1 us; the launch traced here: 70.7 us
  blocking collectives  30.4 us (43%)
  Pallas kernels  20.2 us (28%)
  starting transfers between devices  12.2 us (17%)
  waiting for transfers between devices  7.31 us (10%)
    all_to_all x1, blocking collectives, local(): message = lax.all_to_all(targets, 'grp', 0, 0, tiled=True)  17.5 us
    pallas_call x1, Pallas kernels, interact(): pl.pallas_call(lambda *refs: main_kernel(*refs, active=active), out_shape...  15 us
    all_to_all x1, blocking collectives, local(): parts = lax.all_to_all(result, 'grp', 0, 0, tiled=True)  12.9 us
    all_to_all x1, starting transfers between devices, local(): gathered = lax.all_to_all(sources, 'blk', 0, 0, tiled=True)  12.2 us
    all_to_all x1, waiting for transfers between devices, local(): gathered = lax.all_to_all(sources, 'blk', 0, 0, tiled=True)  7.31 us
    pallas_call x1, Pallas kernels, interact(): pl.pallas_call(lambda *refs: own_kernel(*refs, active=active), out_shape=...  2.97 us
    pallas_call x1, Pallas kernels, local(): pl.pallas_call(prologue_kernel, out_shape=(shape(6, stars), shape(blocks,...  1.54 us
  transfers between devices with their start and end apart: 1, of which 1 were waited for; matrix products, arithmetic and copies ran while one was open for 0% of the time, Pallas kernels for 4%

profile of v4, /device:TPU:1, one launch (start us, length us, event | category | flops | bytes accessed | tf_op | source)
XLA Modules:
  0.0 70.7 jit_solution(14597471406184495981)
XLA Ops:
  0.6 1.5 %prologue.1 = (f32[6,512]{1,0:T(8,128)}, f32[16,8,512]{2,1,0:T(8,128)}, f32[32,128]{1,0:T(8,128)S(1)}, f32[8,512]{1,0:T(8,128)S(1)}) custom-call(s32[1]{0:T(128)} %bitcast.first, s32[1,16]{1,0:T(1,128)} %bitcast.19, f32[3,512]{1,0:T(4,128)} %position.1, f32[3,512]{1,0:T(4,128)} %velocity.1, f32[3,512]{1,0:T(4,128)} %accel_old.1, f32[3,512]{1,0:T(4,128)} %jerk_old.1, ...), custom_call_target="tpu_custom_call" | custom-call | tf_op jit(solution)/shard_map/prologue/pallas_call | solution.py:304
  2.2 17.5 %all_to_all.27 = f32[32,1,128]{2,1,0:T(1,128)S(1)} all-to-all(f32[32,1,128]{2,1,0:T(1,128)S(1)} %bitcast.16), channel_id=1, replica_groups=mesh['blk'=16,'grp'=32] {'grp'}, dimensions={0} | all-to-all | bytes 32768 | tf_op jit(solution)/shard_map/all_to_all | solution.py:310
  19.7 12.2 %all-to-all-start = ((f32[16,8,512]{2,1,0:T(8,128)}), f32[16,8,512]{2,1,0:T(8,128)S(1)}, u32[]{:S(2)}, u32[]{:S(2)}) async-start(f32[16,8,512]{2,1,0:T(8,128)} %get-tuple-element.15), calls=%async_computation | async-start | bytes 524288 | tf_op jit(solution)/shard_map/all_to_all | solution.py:311
  31.8 3.0 %own.1 = (f32[8,512]{1,0:T(8,128)S(1)}, f32[8,512]{1,0:T(8,128)S(1)}, f32[8,128]{1,0:T(8,128)S(1)}, f32[4,24,128]{2,1,0:T(8,128)S(1)}, bf16[128,512]{1,0:T(8,128)(2,1)S(1)}) custom-call(f32[8,512]{1,0:T(8,128)S(1)} %get-tuple-element.16.refs_0_, f32[32,128]{1,0:T(8,128)S(1)} %bitcast.14), custom_call_target="tpu_custom_call" | custom-call | tf_op jit(solution)/shard_map/own/pallas_call | solution.py:327
  34.8 7.3 %all-to-all-done.refs_1_ = f32[16,8,512]{2,1,0:T(8,128)S(1)} async-done(((f32[16,8,512]{2,1,0:T(8,128)}), f32[16,8,512]{2,1,0:T(8,128)S(1)}, u32[]{:S(2)}, u32[]{:S(2)}) %all-to-all-start) | async-done | bytes 262176 | tf_op jit(solution)/shard_map/all_to_all | solution.py:311
  42.1 15.0 %interact.1 = f32[32,128]{1,0:T(8,128)S(1)} custom-call(s32[1]{0:T(128)} %bitcast.4.refs_0_, f32[16,8,512]{2,1,0:T(8,128)S(1)} %all-to-all-done.refs_1_, f32[8,512]{1,0:T(8,128)S(1)} %get-tuple-element.18.refs_2_, f32[8,512]{1,0:T(8,128)S(1)} %get-tuple-element.19.refs_3_, f32[8,128]{1,0:T(8,128)S(1)} %get-tuple-element.20.refs_4_, ...), custom_call_target="tpu_custom_call" | custom-call | tf_op jit(solution)/shard_map/interact/pallas_call | solution.py:333
  57.1 12.9 %all_to_all.28 = f32[32,1,128]{2,1,0:T(1,128)S(1)} all-to-all(f32[32,1,128]{2,1,0:T(1,128)S(1)} %bitcast.13), channel_id=1, replica_groups=mesh['blk'=16,'grp'=32] {'grp'}, dimensions={0} | all-to-all | bytes 32768 | tf_op jit(solution)/shard_map/all_to_all | solution.py:313
  70.1 0.7 final.1
Async XLA Ops:
  19.7 22.5 %all-to-all-start = ((f32[16,8,512]{2,1,0:T(8,128)}), f32[16,8,512]{2,1,0:T(8,128)S(1)}, u32[]{:S(2)}, u32[]{:S(2)}) async-start(f32[16,8,512]{2,1,0:T(8,128)} %get-tuple-element.15), calls=%async_computation | async-start | bytes 524288 | tf_op jit(solution)/shard_map/all_to_all | solution.py:311

commit v5 on v4

--- a/solution.py
+++ b/solution.py
@@ -219,8 +219,7 @@
         chunk = lax.rem(block[0] + 1 + turn, blocks)
         here = sources[chunk]
         scaled = (here - center[:, :1]) * here[7:8]
-        high, middle, low = in_three(scaled)
-        stacked = jnp.concatenate([high.astype(F32), middle.astype(F32), low.astype(F32), jnp.zeros_like(scaled)], 0).astype(BF16)
+        stacked = jnp.concatenate([*three_parts(scaled), jnp.zeros_like(scaled)], 0).astype(BF16)
         radial = source_features(here).T.astype(BF16)
         for step in range(stars // STEP):
             spread_columns(here[:, step * STEP : step * STEP + STEP], spread.at[step], (0, 1, 2))
@@ -261,7 +260,7 @@
                 sum_d[:, lanes] += jnp.dot(left, right_d, preferred_element_type=F32)
         return unused
 
-    lax.fori_loop(0, blocks - 1, one_block, 0, unroll=5)
+    lax.fori_loop(0, blocks - 1, one_block, 0, unroll=15)
     total_w = sum_w[0:8] + (sum_w[8:16] + sum_w[16:24])
     total_d = sum_d[0:8] + (sum_d[8:16] + sum_d[16:24])
     here = [here_rows[k : k + 1] for k in (0, 1, 2, 4, 5, 6)]

time: 71.1 us -> 70.4 us (level)
  no operation moved by 1% of the time
where the time goes in v5:
time: 70.4 us; the launch traced here: 70.1 us
  blocking collectives  30.4 us (43%)
  Pallas kernels  19.5 us (28%)
  starting transfers between devices  12.2 us (17%)
  waiting for transfers between devices  7.31 us (10%)
    all_to_all x1, blocking collectives, local(): message = lax.all_to_all(targets, 'grp', 0, 0, tiled=True)  17.5 us
    pallas_call x1, Pallas kernels, interact(): pl.pallas_call(lambda *refs: main_kernel(*refs, active=active), out_shape...  14.4 us
    all_to_all x1, blocking collectives, local(): parts = lax.all_to_all(result, 'grp', 0, 0, tiled=True)  12.9 us
    all_to_all x1, starting transfers between devices, local(): gathered = lax.all_to_all(sources, 'blk', 0, 0, tiled=True)  12.2 us
    all_to_all x1, waiting for transfers between devices, local(): gathered = lax.all_to_all(sources, 'blk', 0, 0, tiled=True)  7.31 us
    pallas_call x1, Pallas kernels, interact(): pl.pallas_call(lambda *refs: own_kernel(*refs, active=active), out_shape=...  2.97 us
    pallas_call x1, Pallas kernels, local(): pl.pallas_call(prologue_kernel, out_shape=(shape(6, stars), shape(blocks,...  1.54 us
  transfers between devices with their start and end apart: 1, of which 1 were waited for; matrix products, arithmetic and copies ran while one was open for 0% of the time, Pallas kernels for 4%

profile of v5, /device:TPU:1, one launch (start us, length us, event | category | flops | bytes accessed | tf_op | source)
XLA Modules:
  0.0 70.1 jit_solution(17510744113560838262)
XLA Ops:
  0.6 1.5 %prologue.1 = (f32[6,512]{1,0:T(8,128)}, f32[16,8,512]{2,1,0:T(8,128)}, f32[32,128]{1,0:T(8,128)S(1)}, f32[8,512]{1,0:T(8,128)S(1)}) custom-call(s32[1]{0:T(128)} %bitcast.first, s32[1,16]{1,0:T(1,128)} %bitcast.19, f32[3,512]{1,0:T(4,128)} %position.1, f32[3,512]{1,0:T(4,128)} %velocity.1, f32[3,512]{1,0:T(4,128)} %accel_old.1, f32[3,512]{1,0:T(4,128)} %jerk_old.1, ...), custom_call_target="tpu_custom_call" | custom-call | tf_op jit(solution)/shard_map/prologue/pallas_call | solution.py:303
  2.2 17.5 %all_to_all.27 = f32[32,1,128]{2,1,0:T(1,128)S(1)} all-to-all(f32[32,1,128]{2,1,0:T(1,128)S(1)} %bitcast.16), channel_id=1, replica_groups=mesh['blk'=16,'grp'=32] {'grp'}, dimensions={0} | all-to-all | bytes 32768 | tf_op jit(solution)/shard_map/all_to_all | solution.py:309
  19.7 12.2 %all-to-all-start = ((f32[16,8,512]{2,1,0:T(8,128)}), f32[16,8,512]{2,1,0:T(8,128)S(1)}, u32[]{:S(2)}, u32[]{:S(2)}) async-start(f32[16,8,512]{2,1,0:T(8,128)} %get-tuple-element.15), calls=%async_computation | async-start | bytes 524288 | tf_op jit(solution)/shard_map/all_to_all | solution.py:310
  31.8 3.0 %own.1 = (f32[8,512]{1,0:T(8,128)S(1)}, f32[8,512]{1,0:T(8,128)S(1)}, f32[8,128]{1,0:T(8,128)S(1)}, f32[4,24,128]{2,1,0:T(8,128)S(1)}, bf16[128,512]{1,0:T(8,128)(2,1)S(1)}) custom-call(f32[8,512]{1,0:T(8,128)S(1)} %get-tuple-element.16.refs_0_, f32[32,128]{1,0:T(8,128)S(1)} %bitcast.14), custom_call_target="tpu_custom_call" | custom-call | tf_op jit(solution)/shard_map/own/pallas_call | solution.py:326
  34.8 7.3 %all-to-all-done.refs_1_ = f32[16,8,512]{2,1,0:T(8,128)S(1)} async-done(((f32[16,8,512]{2,1,0:T(8,128)}), f32[16,8,512]{2,1,0:T(8,128)S(1)}, u32[]{:S(2)}, u32[]{:S(2)}) %all-to-all-start) | async-done | bytes 262176 | tf_op jit(solution)/shard_map/all_to_all | solution.py:310
  42.1 14.4 %interact.1 = f32[32,128]{1,0:T(8,128)S(1)} custom-call(s32[1]{0:T(128)} %bitcast.4.refs_0_, f32[16,8,512]{2,1,0:T(8,128)S(1)} %all-to-all-done.refs_1_, f32[8,512]{1,0:T(8,128)S(1)} %get-tuple-element.18.refs_2_, f32[8,512]{1,0:T(8,128)S(1)} %get-tuple-element.19.refs_3_, f32[8,128]{1,0:T(8,128)S(1)} %get-tuple-element.20.refs_4_, ...), custom_call_target="tpu_custom_call" | custom-call | tf_op jit(solution)/shard_map/interact/pallas_call | solution.py:332
  56.5 12.9 %all_to_all.28 = f32[32,1,128]{2,1,0:T(1,128)S(1)} all-to-all(f32[32,1,128]{2,1,0:T(1,128)S(1)} %bitcast.13), channel_id=1, replica_groups=mesh['blk'=16,'grp'=32] {'grp'}, dimensions={0} | all-to-all | bytes 32768 | tf_op jit(solution)/shard_map/all_to_all | solution.py:312
  69.4 0.7 final.1
Async XLA Ops:
  19.7 22.5 %all-to-all-start = ((f32[16,8,512]{2,1,0:T(8,128)}), f32[16,8,512]{2,1,0:T(8,128)S(1)}, u32[]{:S(2)}, u32[]{:S(2)}) async-start(f32[16,8,512]{2,1,0:T(8,128)} %get-tuple-element.15), calls=%async_computation | async-start | bytes 524288 | tf_op jit(solution)/shard_map/all_to_all | solution.py:310
